TPU v7x, 32 devices: a whole 2x2x4 slice. The times are simulated.
32 devices in a mesh: row: 2 (over x), col: 4 (over z), layer: 4 (over y, core).
Axes of the slice: x: 2, y: 2, z: 4, core: 2. Of those that a mesh axis runs over, the one named last changes fastest.
Arguments:
- a_blocks: float32 [2, 128, 128, 128], P('row', ('col', 'layer')), may hold values from -0.5 to 0.5
- b_blocks: float32 [32, 4, 128, 128], P(('row', 'layer'), 'col'), may hold values from -5 to 5
- pair_plan: int32 [2, 4, 4, 2, 4, 3, 16], P('row', 'col', 'layer'), may hold values from 0 to 127, as said below
- pair_counts: int32 [2, 4, 4, 2, 4], P('row', 'col', 'layer'), may hold values from 0 to 16, as said below
Outputs:
- next_blocks: float32 [2, 4, 128, 128, 128], P('row', 'col', 'layer')
Inputs may be any that keep to these rules, and one draw needn't show every extreme that they name: `pair_plan`: field 0 names a block of a_blocks whose index divided by 8 (rounded down) is congruent to m modulo 4; field 1 lies in 0 to 3 and field 2 in 0 to 31; entries past the count obey the same ranges. `pair_counts`: some entry equals 16 in every draw.
All inputs are finite; a program needn't handle non-finite values.
Results may differ from a plain program's by a relative error of at most 0.0003.
Values sent between devices are 32-bit elements; how exact they have to be, the bound alone decides.
No kernel may reach another device: no remote copies, remote signals or barrier semaphores. Data moves between devices by JAX's collectives and lax.ppermute only.
A program may use at most 128 MiB of HBM per device.

v0:
```python
import jax
import jax.numpy as jnp
from jax import lax
from jax.sharding import PartitionSpec as P

BS = 128
ACAP = 8
BCAP = 4
CL = 32


def add_pairs(totals, left_blocks, right_blocks, left_ids, right_ids, target, live):
    lhs = jnp.take(left_blocks, left_ids, axis=0)
    rhs = jnp.take(right_blocks, right_ids, axis=0)
    products = jnp.einsum("pij,pjk->pik", lhs, rhs, precision=lax.Precision.HIGHEST)
    products = jnp.where(live[:, None, None], products, jnp.zeros_like(products))
    return totals.at[target].add(products)


def accumulate(totals, left_blocks, right_blocks, entries, numbers, offsets):
    extent = entries.shape[2]
    live = (jnp.arange(extent, dtype=jnp.int32)[None, :] < numbers[:, None]).reshape(-1)
    target = (entries[:, 2] + offsets[:, None]).reshape(-1)
    return add_pairs(
        totals,
        left_blocks,
        right_blocks,
        entries[:, 0].reshape(-1),
        entries[:, 1].reshape(-1),
        target,
        live,
    )


def sweep(totals, piece, groups, group_counts, offsets, left_blocks):
    shards = piece.shape[0] // BCAP

    def per_shard(index, running):
        blocks = lax.dynamic_slice_in_dim(piece, index * BCAP, BCAP, 0)[:, 0]
        entries = lax.dynamic_index_in_dim(groups, index, 0, keepdims=False)
        numbers = lax.dynamic_index_in_dim(group_counts, index, 0, keepdims=False)
        return accumulate(running, left_blocks, blocks, entries, numbers, offsets)

    return lax.fori_loop(0, shards, per_shard, totals)


def per_device(a_blocks, b_blocks, pair_plan, pair_counts):
    layer_count = lax.axis_size("layer")
    plan = pair_plan[0, 0, 0]
    counts = pair_counts[0, 0, 0]
    plan_here, counts_here = (
        lax.all_to_all(plan, "layer", split_axis=1, concat_axis=1, tiled=True),
        lax.all_to_all(counts, "layer", split_axis=1, concat_axis=1, tiled=True),
    )
    left_ids = plan_here[:, :, 0]
    local_ids = left_ids // (layer_count * ACAP) * ACAP + left_ids % ACAP
    plan_here = jnp.stack([local_ids, plan_here[:, :, 1], plan_here[:, :, 2]], axis=2)
    left_blocks = lax.all_gather(a_blocks, "col", axis=1, tiled=True)[0]
    offsets = jnp.arange(layer_count, dtype=jnp.int32) * CL
    initial = jnp.zeros((layer_count * CL, BS, BS), jnp.float32)
    partial_value = sweep(
        initial,
        lax.all_gather(b_blocks, "row", axis=0, tiled=True),
        plan_here,
        counts_here,
        offsets,
        left_blocks,
    )
    result = lax.psum_scatter(partial_value, "layer", scatter_dimension=0, tiled=True)
    return result[None, None]


def solution(mesh):
    in_specs = (
        P("row", ("col", "layer"), None, None),
        P(("row", "layer"), "col", None, None),
        P("row", "col", "layer", None, None, None, None),
        P("row", "col", "layer", None, None),
    )
    out_specs = P("row", "col", "layer", None, None)
    return jax.shard_map(
        per_device, mesh=mesh, in_specs=in_specs, out_specs=out_specs, check_vma=False
    )
```

profile of v0, /device:TPU:9, one launch (start us, length us, event | category | flops | bytes accessed | tf_op | source)
XLA Modules:
  0.0 196.8 jit_solution(3696181291050388086)
XLA Ops:
  6.5 0.7 all-gather.2.cloned.1.call-update
  7.3 1.3 copy.11
  8.6 3.9 %all-to-all-start.1 = ((s32[2,4,1]{0,2,1:T(1,128)}), s32[2,4,1]{0,2,1:T(1,128)S(1)}, u32[]{:S(2)}, u32[]{:S(2)}) async-start(s32[2,4,1]{0,2,1:T(1,128)} %copy.11), calls=%async_computation.1 | async-start | bytes 4096 | tf_op jit(solution)/shard_map/all_to_all | solution.py:53
  12.4 1.3 copy.19
  13.7 1.8 all-to-all-done.1
  15.5 3.9 %all-to-all-start = ((s32[2,4,3,16]{3,0,2,1:T(2,128)}), s32[2,4,3,16]{3,0,2,1:T(2,128)S(1)}, u32[]{:S(2)}, u32[]{:S(2)}) async-start(s32[2,4,3,16]{3,0,2,1:T(2,128)} %bitcast.30), calls=%async_computation | async-start | bytes 24576 | tf_op jit(solution)/shard_map/all_to_all | solution.py:52
  19.4 8.7 %all_gather.7 = f32[8,1,128,128]{3,2,1,0:T(8,128)S(1)} all-gather(f32[4,1,128,128]{3,2,1,0:T(8,128)} %param.7), channel_id=1, replica_groups=mesh['row'=2,'col'=4,'layer'=4] {'row'}, dimensions={0}, use_global_device_ids=true | all-gather | bytes 786432 | tf_op jit(solution)/shard_map/all_gather | solution.py:63
  28.2 0.1 copy.12
  28.3 25.6 %all-gather.2.cloned.1.call-done = f32[1,32,128,128]{3,2,0,1:T(8,128)} async-done(((f32[1,8,128,128]{3,2,0,1:T(8,128)}), f32[1,32,128,128]{3,2,0,1:T(8,128)}) %all-gather.2.cloned.1.call-update) | async-done | bytes 2097168 | tf_op jit(solution)/shard_map/all_gather | solution.py:58
  53.9 4.3 %broadcast_in_dim.70 = f32[128,128,128]{2,1,0:T(8,128)} broadcast(f32[]{:T(128)} %constant.128.clone.1), dimensions={} | broadcast | bytes 8388612 | tf_op jit(solution)/shard_map/broadcast_in_dim | solution.py:60
  58.2 59.6 %while.14 = (s32[]{:T(128)}, f32[128,128,128]{2,1,0:T(8,128)}, s32[2,4,3,16]{3,0,2,1:T(2,128)S(1)}, s32[2,4]{1,0:T(2,128)S(1)}, f32[32,128,128]{2,1,0:T(8,128)S(...) while((s32[]{:T(128)}, f32[128,128,128]{2,1,0:T(8,128)}, ...), condition=%wide.region_2.3_spmd.clone, body=%wide.region_0.2_spmd.clone.sunk | while | flops 1614810624 | bytes 42487800 | solution.py:44
  58.3 0.1 lt.176
  58.5 0.1 add.208
  58.6 0.1 squeeze.60
  58.7 0.1 squeeze.64
  58.8 0.1 squeeze.61
  58.8 0.1 squeeze.63
  58.9 0.1 squeeze.62
  59.1 2.7 %gather_fusion = f32[64,128,128]{2,1,0:T(8,128)} fusion(f32[4,128,128]{2,1,0:T(8,128)S(1)} %dynamic-slice_bitcast_fusion.2, s32[1024]{0:T(1024)S(1)} %pad_clamp_fusion.4), kind=kCustom, calls=%fused_computation.1.clone.clone.1 | custom fusion | bytes 8388864 | tf_op jit(solution)/shard_map/while/body/eval_jaxpr/jit(_take)/gather | solution.py:14
  61.8 2.8 %gather_fusion.1 = f32[64,128,128]{2,1,0:T(8,128)} fusion(f32[32,128,128]{2,1,0:T(8,128)S(1)} %get-tuple-element.250, s32[1024]{0:T(1024)S(1)} %pad_clamp_fusion.5), kind=kCustom, calls=%fused_computation.clone.clone.1 | custom fusion | bytes 8388864 | tf_op jit(solution)/shard_map/while/body/eval_jaxpr/jit(_take)/gather | solution.py:13
  64.6 10.1 %broadcast_select_fusion.2 = f32[64,128,128]{2,1,0:T(8,128)} fusion(f32[64,128,128]{2,1,0:T(8,128)} %gather_fusion, pred[64]{0:T(512)(128)(4,1)S(1)} %get-tuple-element.223, f32[64,128,128]{2,1,0:T(8,128)} %gather_fusion.1, pred[64]{0:T(512)(128)(4,1)S(1)} %get-tuple-element.225, pred[64]{0:T(512)(128)(4,1)S(1)} %lt.176), kind=kOutput, calls=%fused_computation.7.clone.1 | convolution fusion | flops 1613758464 | bytes 12583104 | tf_op jit(solution)/shard_map/while/body/eval_jaxpr/pij,pjk->pik/dot_general | solution.py:15
  74.7 13.4 %scatter_fusion = f32[128,128,128]{2,1,0:T(8,128)} fusion(f32[128,128,128]{2,1,0:T(8,128)} %get-tuple-element.237, s32[64]{0:T(128)S(1)} %get-tuple-element.221, f32[64,128,128]{2,1,0:T(8,128)} %broadcast_select_fusion.2), kind=kCustom, calls=%fused_computation.2.clone.clone.1 | custom fusion | flops 1048576 | bytes 12583168 | tf_op jit(solution)/shard_map/while/body/eval_jaxpr/scatter-add | solution.py:17
  88.1 0.1 lt.176
  88.3 0.1 add.208
  88.4 0.1 squeeze.60
  88.5 0.1 squeeze.64
  88.7 0.1 squeeze.63
  88.9 2.7 %gather_fusion = f32[64,128,128]{2,1,0:T(8,128)} fusion(f32[4,128,128]{2,1,0:T(8,128)S(1)} %dynamic-slice_bitcast_fusion.2, s32[1024]{0:T(1024)S(1)} %pad_clamp_fusion.4), kind=kCustom, calls=%fused_computation.1.clone.clone.1 | custom fusion | bytes 8388864 | tf_op jit(solution)/shard_map/while/body/eval_jaxpr/jit(_take)/gather | solution.py:14
  91.7 2.8 %gather_fusion.1 = f32[64,128,128]{2,1,0:T(8,128)} fusion(f32[32,128,128]{2,1,0:T(8,128)S(1)} %get-tuple-element.250, s32[1024]{0:T(1024)S(1)} %pad_clamp_fusion.5), kind=kCustom, calls=%fused_computation.clone.clone.1 | custom fusion | bytes 8388864 | tf_op jit(solution)/shard_map/while/body/eval_jaxpr/jit(_take)/gather | solution.py:13
  94.4 10.1 %broadcast_select_fusion.2 = f32[64,128,128]{2,1,0:T(8,128)} fusion(f32[64,128,128]{2,1,0:T(8,128)} %gather_fusion, pred[64]{0:T(512)(128)(4,1)S(1)} %get-tuple-element.223, f32[64,128,128]{2,1,0:T(8,128)} %gather_fusion.1, pred[64]{0:T(512)(128)(4,1)S(1)} %get-tuple-element.225, pred[64]{0:T(512)(128)(4,1)S(1)} %lt.176), kind=kOutput, calls=%fused_computation.7.clone.1 | convolution fusion | flops 1613758464 | bytes 12583104 | tf_op jit(solution)/shard_map/while/body/eval_jaxpr/pij,pjk->pik/dot_general | solution.py:15
  104.5 13.4 %scatter_fusion = f32[128,128,128]{2,1,0:T(8,128)} fusion(f32[128,128,128]{2,1,0:T(8,128)} %get-tuple-element.237, s32[64]{0:T(128)S(1)} %get-tuple-element.221, f32[64,128,128]{2,1,0:T(8,128)} %broadcast_select_fusion.2), kind=kCustom, calls=%fused_computation.2.clone.clone.1 | custom fusion | flops 1048576 | bytes 12583168 | tf_op jit(solution)/shard_map/while/body/eval_jaxpr/scatter-add | solution.py:17
  117.9 72.1 %reduce-scatter.2.cloned.1.call-done = f32[32,128,128]{2,1,0:T(8,128)} async-done(((f32[128,128,128]{2,1,0:T(8,128)}), f32[32,128,128]{2,1,0:T(8,128)}) %reduce-scatter.2.cloned.1.call-update) | async-done | bytes 2097168 | tf_op jit(solution)/shard_map/reduce_scatter | solution.py:69
  (37 shorter events, 0.7 us)
Async XLA Ops:
  6.5 47.4 %all-gather.2.cloned.1.call-start = ((), (), s32[]{:S(2)}) async-start(), calls=%async_computation.3 | async-start | bytes 2621440 | tf_op jit(solution)/shard_map/all_gather | solution.py:58
  8.6 7.0 %all-to-all-start.1 = ((s32[2,4,1]{0,2,1:T(1,128)}), s32[2,4,1]{0,2,1:T(1,128)S(1)}, u32[]{:S(2)}, u32[]{:S(2)}) async-start(s32[2,4,1]{0,2,1:T(1,128)} %copy.11), calls=%async_computation.1 | async-start | bytes 4096 | tf_op jit(solution)/shard_map/all_to_all | solution.py:53
  15.5 12.7 %all-to-all-start = ((s32[2,4,3,16]{3,0,2,1:T(2,128)}), s32[2,4,3,16]{3,0,2,1:T(2,128)S(1)}, u32[]{:S(2)}, u32[]{:S(2)}) async-start(s32[2,4,3,16]{3,0,2,1:T(2,128)} %bitcast.30), calls=%async_computation | async-start | bytes 24576 | tf_op jit(solution)/shard_map/all_to_all | solution.py:52
  19.4 170.6 %reduce-scatter.2.cloned.1.call-start = ((), (), s32[]{:S(2)}) async-start(), calls=%async_computation.4 | async-start | bytes 10485760 | tf_op jit(solution)/shard_map/reduce_scatter | solution.py:69
  53.9 4.3 %copy-start = (f32[1,32,128,128]{3,2,0,1:T(8,128)S(1)}, f32[1,32,128,128]{3,2,0,1:T(8,128)}, u32[]{:S(2)}) copy-start(f32[1,32,128,128]{3,2,0,1:T(8,128)} %all-gather.2.cloned.1.call-done) | copy-start | bytes 6291460
Sparse Core Ops, SparseCore 0:
  8.9 44.9 all-gather.1
  118.0 71.9 reduce-scatter.1
where the time goes:
time: 199 us; the launch traced here: 197 us
  waiting for transfers between devices  100 us (50%)
  other arithmetic  27 us (14%)
  matrix products  20.2 us (10%)
  local copies, waits for them, and re-layouts  19.4 us (10%)
  between operations  13.4 us (7%)
  blocking collectives  8.73 us (4%)
  starting transfers between devices  7.78 us (4%)
    reduce_scatter x1, waiting for transfers between devices, per_device(): lax.psum_scatter(partial_value, 'layer', scatter_dimension=0, tiled=True)  72.1 us
    scatter-add x2, other arithmetic, add_pairs(): return totals.at[target].add(products)  26.7 us
    all_gather x1, waiting for transfers between devices, per_device(): left_blocks = lax.all_gather(a_blocks, 'col', axis=1, tiled=True)[0]  25.6 us
    dot_general x2, matrix products, add_pairs(): jnp.einsum('pij,pjk->pik', lhs, rhs, precision=lax.Precision.HIGHEST)  20.2 us
    all_gather x1, blocking collectives, per_device(): lax.all_gather(b_blocks, 'row', axis=0, tiled=True)  8.73 us
    gather x2, local copies, waits for them, and re-layouts, add_pairs(): lhs = jnp.take(left_blocks, left_ids, axis=0)  5.51 us
    gather x2, local copies, waits for them, and re-layouts, add_pairs(): rhs = jnp.take(right_blocks, right_ids, axis=0)  5.49 us
    broadcast_in_dim x1, local copies, waits for them, and re-layouts, per_device(): initial = jnp.zeros((layer_count * CL, BS, BS), jnp.float32)  4.28 us
  transfers between devices with their start and end apart: 4, of which 3 were waited for; matrix products, arithmetic and copies ran while one was open for 1% of the time, Pallas kernels for 0%

commit v1 on v0

v1 whole, which is shorter than its diff:
```python
import functools

import jax
import jax.numpy as jnp
from jax import lax
from jax.experimental import pallas as pl
from jax.experimental.pallas import tpu as pltpu
from jax.sharding import PartitionSpec as P

CL = 32
UNROLL = 8
F32 = jnp.float32
BF16 = jnp.bfloat16


def sort_kernel(rel_of, stage_of, base_of, a_cap, b_of, plan, counts, lists, sizes, stage_tab, base_tab):
    shards, layers, _, _ = plan.shape
    n_col = stage_tab.shape[0] // layers
    stages = sizes.shape[0]
    room = lists.shape[1]
    z, me = lax.axis_index("col"), lax.axis_index("layer")
    row = lax.axis_index("row")
    rels = sorted({rel for rel, _ in stage_of})
    for zp in range(n_col):
        rel = rel_of(zp, z)
        for dm in range(layers):
            stage = jnp.int32(0)
            base = jnp.int32(0)
            for r in rels:
                stage = jnp.where(rel == r, stage_of[r, dm], stage)
                base = jnp.where(rel == r, base_of[r, dm], base)
            stage_tab[zp * layers + dm] = stage
            base_tab[zp * layers + dm] = base
    for st in range(stages):
        sizes[st] = 0

    def per_list(q, _):
        s, m = q // layers, q % layers
        dm = m ^ me
        b_base = b_of(s, row, dm)

        def per_pair(p, _):
            left = plan[s, m, 0, p]
            at = (left // (layers * a_cap)) * layers + dm
            st = stage_tab[at]
            pos = sizes[st]
            lists[st, pos] = (
                (base_tab[at] + left % a_cap) | ((b_base + plan[s, m, 1, p]) << 10) | (plan[s, m, 2, p] << 20)
            )
            sizes[st] = pos + 1
            return 0

        return lax.fori_loop(0, counts[s, m], per_pair, 0)

    lax.fori_loop(0, shards * layers, per_list, 0)
    for st in range(stages):
        n = sizes[st]
        for u in range(UNROLL - 1):
            lists[st, n + u] = CL << 20
    del room


def halves(x):
    high = x.astype(BF16)
    return high, (x - high.astype(F32)).astype(BF16)


def product(a, b):
    ah, al = halves(a)
    bh, bl = halves(b)
    dot = functools.partial(jnp.dot, preferred_element_type=F32)
    return dot(ah, bh) + (dot(al, bh) + dot(ah, bl))


def stage_kernel(stage, a_at, n_a, n_b, carried, *refs):
    sizes, lists = refs[:2]
    a_refs = refs[2 : 2 + n_a]
    b_refs = refs[2 + n_a : 2 + n_a + n_b]
    rest = refs[2 + n_a + n_b :]
    if carried:
        acc_in, out, a_buf, b_buf, acc, sems = rest
    else:
        out, a_buf, b_buf, acc, sems = rest
    copies = []
    at = 0
    for ref in b_refs:
        n = ref.shape[0]
        copies.append(pltpu.make_async_copy(ref, b_buf.at[pl.ds(at, n)], sems.at[len(copies)]))
        at += n
    for ref, (at, n) in zip(a_refs, a_at):
        copies.append(pltpu.make_async_copy(ref.at[pl.ds(0, n)], a_buf.at[pl.ds(at, n)], sems.at[len(copies)]))
    if carried:
        copies.append(pltpu.make_async_copy(acc_in, acc.at[pl.ds(0, CL)], sems.at[len(copies)]))
    for copy in copies:
        copy.start()
    if carried:
        acc[CL] = jnp.zeros(acc.shape[1:], F32)
    else:
        acc[...] = jnp.zeros(acc.shape, F32)
    for copy in copies:
        copy.wait()

    def body(i, _):
        terms = []
        for u in range(UNROLL):
            entry = lists[stage, i * UNROLL + u]
            terms.append((entry >> 20, product(a_buf[entry & 1023], b_buf[(entry >> 10) & 1023])))
        for target, term in terms:
            acc[target] = acc[target] + term
        return 0

    lax.fori_loop(0, (sizes[stage] + UNROLL - 1) // UNROLL, body, 0)
    done = pltpu.make_async_copy(acc.at[pl.ds(0, CL)], out, sems.at[0])
    done.start()
    done.wait()


def run_stage(stage, sizes, lists, a_parts, b_parts, acc):
    bs = b_parts[0].shape[1:]
    n_blocks = max(at + n for _, at, n in a_parts)
    b_blocks = sum(b.shape[0] for b in b_parts)
    anywhere = pl.BlockSpec(memory_space=pl.ANY)
    smem = pl.BlockSpec(memory_space=pltpu.SMEM)
    arrays = [a for a, _, _ in a_parts] + list(b_parts) + ([] if acc is None else [acc])
    pairs = lists.shape[1] // 2
    return pl.pallas_call(
        functools.partial(
            stage_kernel, stage, [(at, n) for _, at, n in a_parts], len(a_parts), len(b_parts), acc is not None
        ),
        out_shape=jax.ShapeDtypeStruct((CL,) + bs, F32),
        in_specs=[smem, smem] + [anywhere] * len(arrays),
        out_specs=anywhere,
        scratch_shapes=[
            pltpu.VMEM((n_blocks,) + bs, F32),
            pltpu.VMEM((b_blocks,) + bs, F32),
            pltpu.VMEM((CL + 1,) + bs, F32),
            pltpu.SemaphoreType.DMA((len(arrays),)),
        ],
        cost_estimate=pl.CostEstimate(
            flops=6 * pairs * bs[0] * bs[0] * bs[1], bytes_accessed=4 * bs[0] * bs[1] * 80, transcendentals=0
        ),
        name=f"stage_{stage}",
    )(sizes, lists, *arrays)


def per_device(a_blocks, b_blocks, pair_plan, pair_counts):
    n_row, n_col, n_layer = (lax.axis_size(x) for x in ("row", "col", "layer"))
    z = lax.axis_index("col")
    own, b_own = a_blocks[0], b_blocks[:, 0]
    a_cap, b_cap = own.shape[0], b_own.shape[0]
    plan, counts = pair_plan[0, 0, 0], pair_counts[0, 0, 0]
    half = n_layer // 2

    def over_layer(x, d):
        return lax.ppermute(x, "layer", [(i, i ^ d) for i in range(n_layer)])

    def over_row(x):
        return lax.ppermute(x, "row", [(i, i ^ 1) for i in range(n_row)])

    def pairs_end(x):
        return lax.ppermute(x, "col", [(i, i ^ 1) for i in range(n_col)])

    def pairs_mid(x):
        moves = []
        for c in range(n_col):
            inner = 0 < c < n_col - 1
            for m in range(n_layer):
                to = (c - 1 if c % 2 == 0 else c + 1, m) if inner else (c, m ^ 1)
                moves.append((c * n_layer + m, to[0] * n_layer + to[1]))
        return lax.ppermute(x, ("col", "layer"), moves)

    is_end = jnp.logical_or(z == 0, z == n_col - 1)
    g = a_cap * 3 // 4
    y_own = over_layer(own, half)
    p_a = pairs_end(own)
    p_b = pairs_mid(own)
    y_b = over_layer(b_own, half)
    x_b = over_row(b_own)
    q = pairs_mid(p_a)
    r = pairs_end(p_b)
    y_a = over_layer(p_a[g:], half)
    x2 = jnp.where(is_end, r, p_b)
    y_2 = over_layer(x2, half)
    x_yb = over_row(y_b)
    t = pairs_end(q)
    x3 = jnp.where(is_end, t, q)
    y_3 = over_layer(x3, half)
    p_y = pairs_end(y_own[:g])

    stages = [
        [((0, 0), [own]), ((1, 0), [p_a]), ((0, half), [y_own])],
        [((2, 0), [x2]), ((3, 0), [x3]), ((1, half), [p_y, y_a]), ((2, half), [y_2])],
        [((3, half), [y_3])],
    ]
    stage_of, base_of, a_parts = {}, {}, []
    for st, groups in enumerate(stages):
        at, parts = 0, []
        for (rel, dm), arrays in groups:
            for other in (0, 1):
                stage_of[rel, dm ^ other], base_of[rel, dm ^ other] = st, at
                for x in arrays:
                    parts.append((over_layer(x, 1) if other else x, at, x.shape[0]))
                    at += x.shape[0]
        a_parts.append(parts)

    b_parts = []
    for x in (b_own, x_b, y_b, x_yb):
        b_parts += [x, over_layer(x, 1)]

    def b_of(s, row, dm):
        return ((dm // half) * 4 + (s ^ row) * 2 + dm % half) * b_cap

    def rel_of(zp, z):
        far = jnp.int32(3 if zp in (0, n_col - 1) else 2)
        return jnp.where(z == zp, 0, jnp.where(z == zp ^ 1, 1, far))

    shards, layers, _, p_cap = plan.shape
    room = shards * layers * p_cap + UNROLL
    smem = pl.BlockSpec(memory_space=pltpu.SMEM)
    lists, sizes = pl.pallas_call(
        functools.partial(sort_kernel, rel_of, stage_of, base_of, a_cap, b_of),
        out_shape=(
            jax.ShapeDtypeStruct((len(stages), room), jnp.int32),
            jax.ShapeDtypeStruct((len(stages),), jnp.int32),
        ),
        in_specs=[smem, smem],
        out_specs=(smem, smem),
        scratch_shapes=[pltpu.SMEM((n_col * layers,), jnp.int32), pltpu.SMEM((n_col * layers,), jnp.int32)],
        name="sort_pairs",
    )(plan, counts)
    acc = None
    for st, parts in enumerate(a_parts):
        acc = run_stage(st, sizes, lists, parts, b_parts, acc)
    return acc[None, None]


def solution(mesh):
    in_specs = (
        P("row", ("col", "layer"), None, None),
        P(("row", "layer"), "col", None, None),
        P("row", "col", "layer", None, None, None, None),
        P("row", "col", "layer", None, None),
    )
    out_specs = P("row", "col", "layer", None, None)
    return jax.shard_map(
        per_device, mesh=mesh, in_specs=in_specs, out_specs=out_specs, check_vma=False
    )
```

time: 199 us -> 95.7 us (0.48)
  waiting for transfers between devices: 100 us -> 37.7 us
  other arithmetic: 27 us -> 2.2 us
  Pallas kernels: 0 us -> 24.3 us
  starting transfers between devices: 7.78 us -> 28.2 us
  matrix products: 20.2 us -> 0 us
  local copies, waits for them, and re-layouts: 19.4 us -> 2.3 us
  between operations: 13.4 us -> 0.29 us
  blocking collectives: 8.73 us -> 0 us
    reduce_scatter x1 -> x0, waiting for transfers between devices: 72.1 us -> none  [per_device(): lax.psum_scatter(partial_value, 'layer', scatter_dimension=0, tiled=True)]
    ppermute x0 -> x26, waiting for transfers between devices: none -> 37.7 us  [the longest x4 19.5 us: pairs_end(): return lax.ppermute(x, 'col', [(i, i ^ 1) for i in range(n_col)])]
    ppermute x0 -> x26, starting transfers between devices: none -> 28.2 us  [the longest x18 21 us: over_layer(): return lax.ppermute(x, 'layer', [(i, i ^ d) for i in range(n_layer)])]
    scatter-add x2 -> x0, other arithmetic: 26.7 us -> none  [add_pairs(): return totals.at[target].add(products)]
    all_gather x1 -> x0, waiting for transfers between devices: 25.6 us -> none  [per_device(): left_blocks = lax.all_gather(a_blocks, 'col', axis=1, tiled=True)[0]]
    pallas_call x0 -> x4, Pallas kernels: none -> 24.3 us  [the longest x3 20.1 us: run_stage(): pl.pallas_call(functools.partial(stage_kernel, stage, [(at, n) for _, at,...]
    dot_general x2 -> x0, matrix products: 20.2 us -> none  [add_pairs(): jnp.einsum('pij,pjk->pik', lhs, rhs, precision=lax.Precision.HIGHEST)]
    gather x4 -> x0, local copies, waits for them, and re-layouts: 11 us -> none  [the longest x2 5.51 us: add_pairs(): lhs = jnp.take(left_blocks, left_ids, axis=0)]
  transfers between devices with their start and end apart: 4 -> 26, of which waited for: 3 -> 8; matrix products, arithmetic and copies ran while one was open for 1% -> 3% of each run, Pallas kernels for 0% -> 20%
where the time goes in v1:
time: 95.7 us; the launch traced here: 95 us
  waiting for transfers between devices  37.7 us (39%)
  starting transfers between devices  28.2 us (29%)
  Pallas kernels  24.3 us (25%)
  local copies, waits for them, and re-layouts  2.3 us (2%)
  other arithmetic  2.2 us (2%)
    ppermute x18, starting transfers between devices, over_layer(): return lax.ppermute(x, 'layer', [(i, i ^ d) for i in range(n_layer)])  21 us
    pallas_call x3, Pallas kernels, run_stage(): pl.pallas_call(functools.partial(stage_kernel, stage, [(at, n) for _, at,...  20.1 us
    ppermute x4, waiting for transfers between devices, pairs_end(): return lax.ppermute(x, 'col', [(i, i ^ 1) for i in range(n_col)])  19.5 us
    ppermute x18, waiting for transfers between devices, over_layer(): return lax.ppermute(x, 'layer', [(i, i ^ d) for i in range(n_layer)])  17.2 us
    pallas_call x1, Pallas kernels, per_device(): pl.pallas_call(functools.partial(sort_kernel, rel_of, stage_of, base_of,...  4.26 us
    ppermute x2, starting transfers between devices, pairs_mid(): return lax.ppermute(x, ('col', 'layer'), moves)  3.89 us
    ppermute x2, starting transfers between devices, over_row(): return lax.ppermute(x, 'row', [(i, i ^ 1) for i in range(n_row)])  2.42 us
    unnamed x43, local copies, waits for them, and re-layouts  2.26 us
  transfers between devices with their start and end apart: 26, of which 8 were waited for; matrix products, arithmetic and copies ran while one was open for 3% of the time, Pallas kernels for 20%

profile of v1, /device:TPU:9, one launch (start us, length us, event | category | flops | bytes accessed | tf_op | source)
XLA Modules:
  0.0 95.0 jit_solution(17339414030924733451)
XLA Ops:
  0.0 2.6 %collective-permute-start.12 = (f32[8,128,128]{2,1,0:T(8,128)}, f32[8,128,128]{2,1,0:T(8,128)S(1)}, u32[]{:S(2)}, u32[]{:S(2)}) collective-permute-start(f32[8,128,128]{2,1,0:T(8,128)} %bitcast.14), channel_id=1, source_target_pairs={{0,1},{1,0},{2,3},{3,2},{4,8},{5,9},{6,10},{7,11},{8,4},{9,5},{10,... | collective-permute-start | bytes 1572872 | tf_op jit(solution)/shard_map/ppermute | solution.py:170
  2.6 10.4 %collective-permute-done.refs_4_ = f32[8,128,128]{2,1,0:T(8,128)S(1)} collective-permute-done((f32[8,128,128]{2,1,0:T(8,128)}, f32[8,128,128]{2,1,0:T(8,128)S(1)}, u32[]{:S(2)}, u32[]{:S(2)}) %collective-permute-start) | collective-permute-done | bytes 524320 | tf_op jit(solution)/shard_map/ppermute | solution.py:161
  13.0 1.3 %collective-permute-start.1 = (f32[8,128,128]{2,1,0:T(8,128)S(1)}, f32[8,128,128]{2,1,0:T(8,128)S(1)}, u32[]{:S(2)}, u32[]{:S(2)}) collective-permute-start(f32[8,128,128]{2,1,0:T(8,128)S(1)} %collective-permute-done.refs_4_), channel_id=1, source_target_pairs={{0,1},{1,0},{2,3},{3,2},{4,8},{5,9},{6,10},{7,11},{8,4},{9,5},{10,... | collective-permute-start | bytes 1572872 | tf_op jit(solution)/shard_map/ppermute | solution.py:170
  14.3 1.2 %collective-permute-start.8 = (f32[4,128,128]{2,1,0:T(8,128)}, f32[4,128,128]{2,1,0:T(8,128)S(1)}, u32[]{:S(2)}, u32[]{:S(2)}) collective-permute-start(f32[4,128,128]{2,1,0:T(8,128)} %bitcast.7), channel_id=1, source_target_pairs={{0,2},{1,3},{2,0},{3,1},{4,6},{5,7},{6,4},{7,5},{8,10},{9,11},{10,... | collective-permute-start | bytes 786440 | tf_op jit(solution)/shard_map/ppermute | solution.py:155
  15.6 1.2 %collective-permute-start.6 = (f32[4,128,128]{2,1,0:T(8,128)}, f32[4,128,128]{2,1,0:T(8,128)S(1)}, u32[]{:S(2)}, u32[]{:S(2)}) collective-permute-start(f32[4,128,128]{2,1,0:T(8,128)} %bitcast.8), channel_id=1, source_target_pairs={{0,16},{16,0},{1,17},{17,1},{2,18},{18,2},{3,19},{19,3},{4,20},{20... | collective-permute-start | bytes 786440 | tf_op jit(solution)/shard_map/ppermute | solution.py:158
  17.2 2.0 %collective-permute-start.5 = (f32[4,128,128]{2,1,0:T(8,128)}, f32[4,128,128]{2,1,0:T(8,128)S(1)}, u32[]{:S(2)}, u32[]{:S(2)}) collective-permute-start(f32[4,128,128]{2,1,0:T(8,128)} %bitcast.9), channel_id=1, source_target_pairs={{0,1},{1,0},{2,3},{3,2},{4,5},{5,4},{6,7},{7,6},{8,9},{9,8},{10,11... | collective-permute-start | bytes 786440 | tf_op jit(solution)/shard_map/ppermute | solution.py:155
  19.2 1.4 %collective-permute-done.8.refs_12_.refs_16_.refs_8_ = f32[4,128,128]{2,1,0:T(8,128)S(1)} collective-permute-done((f32[4,128,128]{2,1,0:T(8,128)}, f32[4,128,128]{2,1,0:T(8,128)S(1)}, u32[]{:S(2)}, u32[]{:S(2)}) %collective-permute-start.8) | collective-permute-done | bytes 262176 | tf_op jit(solution)/shard_map/ppermute | solution.py:155
  20.6 1.2 %collective-permute-start.10 = (f32[4,128,128]{2,1,0:T(8,128)S(1)}, f32[4,128,128]{2,1,0:T(8,128)S(1)}, u32[]{:S(2)}, u32[]{:S(2)}) collective-permute-start(f32[4,128,128]{2,1,0:T(8,128)S(1)} %collective-permute-done.8.refs_12_.refs_16_.refs_8_), channel_id=1, source_target_pairs={{0,16},{16,0},{1,17},{17,1},{2,18},{18,2},{3,19},{19,3},{4,20},{20... | collective-permute-start | bytes 786440 | tf_op jit(solution)/shard_map/ppermute | solution.py:158
  21.8 3.5 %collective-permute-start.9 = (f32[4,128,128]{2,1,0:T(8,128)S(1)}, f32[4,128,128]{2,1,0:T(8,128)S(1)}, u32[]{:S(2)}, u32[]{:S(2)}) collective-permute-start(f32[4,128,128]{2,1,0:T(8,128)S(1)} %collective-permute-done.8.refs_12_.refs_16_.refs_8_), channel_id=1, source_target_pairs={{0,1},{1,0},{2,3},{3,2},{4,5},{5,4},{6,7},{7,6},{8,9},{9,8},{10,11... | collective-permute-start | bytes 786440 | tf_op jit(solution)/shard_map/ppermute | solution.py:155
  26.4 1.1 %collective-permute-done.10.refs_14_.refs_18_.refs_10_ = f32[4,128,128]{2,1,0:T(8,128)S(1)} collective-permute-done((f32[4,128,128]{2,1,0:T(8,128)S(1)}, f32[4,128,128]{2,1,0:T(8,128)S(1)}, u32[]{:S(2)}, u32[]{:S(2)}) %collective-permute-start.10) | collective-permute-done | bytes 262176 | tf_op jit(solution)/shard_map/ppermute | solution.py:158
  27.5 2.6 %collective-permute-start.23 = (f32[8,128,128]{2,1,0:T(8,128)}, f32[8,128,128]{2,1,0:T(8,128)S(1)}, u32[]{:S(2)}, u32[]{:S(2)}) collective-permute-start(f32[8,128,128]{2,1,0:T(8,128)} %bitcast.16), channel_id=1, source_target_pairs={{0,1},{1,0},{2,3},{3,2},{4,5},{5,4},{6,7},{7,6},{8,9},{9,8},{10,11... | collective-permute-start | bytes 1572872 | tf_op jit(solution)/shard_map/ppermute | solution.py:155
  30.2 0.8 collective-permute-start.18
  31.0 1.1 %broadcast_select_fusion.refs_2_ = f32[8,128,128]{2,1,0:T(8,128)S(1)} fusion(f32[8,128,128]{2,1,0:T(8,128)} %collective-permute-done.13, f32[8,128,128]{2,1,0:T(8,128)} %copy-done.17, pred[]{:T(512)S(6)} %or.3), kind=kLoop, calls=%fused_computation | loop fusion | flops 131072 | bytes 1572865 | tf_op jit(solution)/shard_map/jit(_where)/select_n | solution.py:182
  32.2 2.2 %collective-permute-start.11 = (f32[4,128,128]{2,1,0:T(8,128)S(1)}, f32[4,128,128]{2,1,0:T(8,128)S(1)}, u32[]{:S(2)}, u32[]{:S(2)}) collective-permute-start(f32[4,128,128]{2,1,0:T(8,128)S(1)} %collective-permute-done.10.refs_14_.refs_18_.refs_10_), channel_id=1, source_target_pairs={{0,1},{1,0},{2,3},{3,2},{4,5},{5,4},{6,7},{7,6},{8,9},{9,8},{10,11... | collective-permute-start | bytes 786440 | tf_op jit(solution)/shard_map/ppermute | solution.py:155
  34.4 4.6 %collective-permute-done.16.refs_6_ = f32[8,128,128]{2,1,0:T(8,128)S(1)} collective-permute-done((f32[8,128,128]{2,1,0:T(8,128)}, f32[8,128,128]{2,1,0:T(8,128)S(1)}, u32[]{:S(2)}, u32[]{:S(2)}) %collective-permute-start.16) | collective-permute-done | bytes 524320 | tf_op jit(solution)/shard_map/ppermute | solution.py:155
  39.0 1.4 %collective-permute-start.25 = (f32[8,128,128]{2,1,0:T(8,128)S(1)}, f32[8,128,128]{2,1,0:T(8,128)S(1)}, u32[]{:S(2)}, u32[]{:S(2)}) collective-permute-start(f32[8,128,128]{2,1,0:T(8,128)S(1)} %collective-permute-done.16.refs_6_), channel_id=1, source_target_pairs={{0,1},{1,0},{2,3},{3,2},{4,5},{5,4},{6,7},{7,6},{8,9},{9,8},{10,11... | collective-permute-start | bytes 1572872 | tf_op jit(solution)/shard_map/ppermute | solution.py:155
  40.4 1.4 %collective-permute-done.18.refs_7_ = f32[2,128,128]{2,1,0:T(8,128)S(1)} collective-permute-done((f32[2,128,128]{2,1,0:T(8,128)S(1)}, f32[2,128,128]{2,1,0:T(8,128)S(1)}, u32[]{:S(2)}, u32[]{:S(2)}) %collective-permute-start.18) | collective-permute-done | bytes 131104 | tf_op jit(solution)/shard_map/ppermute | solution.py:155
  41.8 0.8 collective-permute-start.20
  42.7 0.7 collective-permute-start.21
  43.4 1.1 %broadcast_select_fusion.1.refs_4_ = f32[8,128,128]{2,1,0:T(8,128)S(1)} fusion(f32[8,128,128]{2,1,0:T(8,128)} %collective-permute-done.2, f32[8,128,128]{2,1,0:T(8,128)} %copy-done.16, pred[]{:T(512)S(6)} %or.3), kind=kLoop, calls=%fused_computation.1 | loop fusion | flops 131072 | bytes 1572865 | tf_op jit(solution)/shard_map/jit(_where)/select_n | solution.py:186
  44.5 0.8 collective-permute-start.3
  45.5 1.1 %collective-permute-start.24 = (f32[8,128,128]{2,1,0:T(8,128)S(1)}, f32[8,128,128]{2,1,0:T(8,128)S(1)}, u32[]{:S(2)}, u32[]{:S(2)}) collective-permute-start(f32[8,128,128]{2,1,0:T(8,128)S(1)} %copy-done.11), channel_id=1, source_target_pairs={{0,1},{1,0},{2,3},{3,2},{4,5},{5,4},{6,7},{7,6},{8,9},{9,8},{10,11... | collective-permute-start | bytes 1572872 | tf_op jit(solution)/shard_map/ppermute | solution.py:155
  46.6 9.0 %collective-permute-done.17.refs_6_ = f32[6,128,128]{2,1,0:T(8,128)} collective-permute-done((f32[6,128,128]{2,1,0:T(8,128)S(1)}, f32[6,128,128]{2,1,0:T(8,128)}, u32[]{:S(2)}, u32[]{:S(2)}) %collective-permute-start.17) | collective-permute-done | bytes 393248 | tf_op jit(solution)/shard_map/ppermute | solution.py:161
  55.6 1.5 %collective-permute-start.14 = (f32[8,128,128]{2,1,0:T(8,128)S(1)}, f32[8,128,128]{2,1,0:T(8,128)S(1)}, u32[]{:S(2)}, u32[]{:S(2)}) collective-permute-start(f32[8,128,128]{2,1,0:T(8,128)S(1)} %broadcast_select_fusion.refs_2_), channel_id=1, source_target_pairs={{0,1},{1,0},{2,3},{3,2},{4,5},{5,4},{6,7},{7,6},{8,9},{9,8},{10,11... | collective-permute-start | bytes 1572872 | tf_op jit(solution)/shard_map/ppermute | solution.py:155
  57.7 9.7 %collective-permute-done.3.refs_2_ = f32[8,128,128]{2,1,0:T(8,128)} collective-permute-done((f32[8,128,128]{2,1,0:T(8,128)S(1)}, f32[8,128,128]{2,1,0:T(8,128)}, u32[]{:S(2)}, u32[]{:S(2)}) %collective-permute-start.3) | collective-permute-done | bytes 524320 | tf_op jit(solution)/shard_map/ppermute | solution.py:155
  67.4 0.9 collective-permute-start.4
  68.4 0.8 copy-done.15
  69.8 4.3 %sort_pairs.1 = (s32[3,136]{1,0:T(4,128)}, s32[3]{0:T(128)}) custom-call(s32[2,4,3,16]{3,2,1,0:T(4,128)} %bitcast.18, s32[2,4]{1,0:T(2,128)} %bitcast.19), custom_call_target="tpu_custom_call" | custom-call | tf_op jit(solution)/shard_map/sort_pairs/pallas_call | solution.py:220
  74.1 6.6 %stage_0.1.refs_20_ = f32[32,128,128]{2,1,0:T(8,128)} custom-call(s32[3]{0:T(128)} %get-tuple-element.7.refs_0_, s32[3,136]{1,0:T(4,128)} %get-tuple-element.8.refs_1_, f32[8,128,128]{2,1,0:T(8,128)} %bitcast.17, f32[8,128,128]{2,1,0:T(8,128)} %copy-done.12, f32[8,128,128]{2,1,0:T(8,128)} %copy-done.10, f32[8,128,128]{2,1,0:T(8,128)} %copy-done.15, ...), custom_call_target="tpu_custom_call" | custom-call | flops 855638016 | bytes 5242880 | tf_op jit(solution)/shard_map/stage_0/pallas_call | solution.py:126
  80.7 0.8 copy-done.14
  81.5 8.0 %stage_1.1.refs_12_ = f32[32,128,128]{2,1,0:T(8,128)} custom-call(s32[3]{0:T(128)} %get-tuple-element.7.refs_0_, s32[3,136]{1,0:T(4,128)} %get-tuple-element.8.refs_1_, f32[8,128,128]{2,1,0:T(8,128)} %copy-done.7, f32[8,128,128]{2,1,0:T(8,128)} %copy-done.14, f32[8,128,128]{2,1,0:T(8,128)} %copy-done.8, f32[8,128,128]{2,1,0:T(8,128)} %collective-permute-done.15.refs_5_, ...), custom_call_target="tpu_custom_call" | custom-call | flops 855638016 | bytes 5242880 | tf_op jit(solution)/shard_map/stage_1/pallas_call | solution.py:126
  89.6 5.5 %stage_2.1 = f32[32,128,128]{2,1,0:T(8,128)} custom-call(s32[3]{0:T(128)} %get-tuple-element.7.refs_0_, s32[3,136]{1,0:T(4,128)} %get-tuple-element.8.refs_1_, f32[8,128,128]{2,1,0:T(8,128)} %collective-permute-done.3.refs_2_, f32[8,128,128]{2,1,0:T(8,128)} %collective-permute-done.4.refs_3_, f32[4,128,128]{2,1,0:T(8,128)} %bitcast.12, ...), custom_call_target="tpu_custom_call" | custom-call | flops 855638016 | bytes 5242880 | tf_op jit(solution)/shard_map/stage_2/pallas_call | solution.py:126
  (71 shorter events, 3.1 us)
Async XLA Ops:
  0.0 13.0 %collective-permute-start = (f32[8,128,128]{2,1,0:T(8,128)}, f32[8,128,128]{2,1,0:T(8,128)S(1)}, u32[]{:S(2)}, u32[]{:S(2)}) collective-permute-start(f32[8,128,128]{2,1,0:T(8,128)} %bitcast.13), channel_id=1, source_target_pairs={{0,4},{4,0},{8,12},{12,8},{1,5},{5,1},{9,13},{13,9},{2,6},{6,2},{1... | collective-permute-start | bytes 1572872 | tf_op jit(solution)/shard_map/ppermute | solution.py:161
  0.0 16.8 %collective-permute-start.12 = (f32[8,128,128]{2,1,0:T(8,128)}, f32[8,128,128]{2,1,0:T(8,128)S(1)}, u32[]{:S(2)}, u32[]{:S(2)}) collective-permute-start(f32[8,128,128]{2,1,0:T(8,128)} %bitcast.14), channel_id=1, source_target_pairs={{0,1},{1,0},{2,3},{3,2},{4,8},{5,9},{6,10},{7,11},{8,4},{9,5},{10,... | collective-permute-start | bytes 1572872 | tf_op jit(solution)/shard_map/ppermute | solution.py:170
  13.0 13.0 %collective-permute-start.1 = (f32[8,128,128]{2,1,0:T(8,128)S(1)}, f32[8,128,128]{2,1,0:T(8,128)S(1)}, u32[]{:S(2)}, u32[]{:S(2)}) collective-permute-start(f32[8,128,128]{2,1,0:T(8,128)S(1)} %collective-permute-done.refs_4_), channel_id=1, source_target_pairs={{0,1},{1,0},{2,3},{3,2},{4,8},{5,9},{6,10},{7,11},{8,4},{9,5},{10,... | collective-permute-start | bytes 1572872 | tf_op jit(solution)/shard_map/ppermute | solution.py:170
  14.3 6.3 %collective-permute-start.8 = (f32[4,128,128]{2,1,0:T(8,128)}, f32[4,128,128]{2,1,0:T(8,128)S(1)}, u32[]{:S(2)}, u32[]{:S(2)}) collective-permute-start(f32[4,128,128]{2,1,0:T(8,128)} %bitcast.7), channel_id=1, source_target_pairs={{0,2},{1,3},{2,0},{3,1},{4,6},{5,7},{6,4},{7,5},{8,10},{9,11},{10,... | collective-permute-start | bytes 786440 | tf_op jit(solution)/shard_map/ppermute | solution.py:155
  15.6 6.2 %collective-permute-start.6 = (f32[4,128,128]{2,1,0:T(8,128)}, f32[4,128,128]{2,1,0:T(8,128)S(1)}, u32[]{:S(2)}, u32[]{:S(2)}) collective-permute-start(f32[4,128,128]{2,1,0:T(8,128)} %bitcast.8), channel_id=1, source_target_pairs={{0,16},{16,0},{1,17},{17,1},{2,18},{18,2},{3,19},{19,3},{4,20},{20... | collective-permute-start | bytes 786440 | tf_op jit(solution)/shard_map/ppermute | solution.py:158
  16.8 13.4 %collective-permute-start.13 = (f32[8,128,128]{2,1,0:T(8,128)S(1)}, f32[8,128,128]{2,1,0:T(8,128)}, u32[]{:S(2)}, u32[]{:S(2)}) collective-permute-start(f32[8,128,128]{2,1,0:T(8,128)S(1)} %collective-permute-done.12), channel_id=1, source_target_pairs={{0,4},{4,0},{8,12},{12,8},{1,5},{5,1},{9,13},{13,9},{2,6},{6,2},{1... | collective-permute-start | bytes 1572872 | tf_op jit(solution)/shard_map/ppermute | solution.py:161
  17.2 8.1 %collective-permute-start.5 = (f32[4,128,128]{2,1,0:T(8,128)}, f32[4,128,128]{2,1,0:T(8,128)S(1)}, u32[]{:S(2)}, u32[]{:S(2)}) collective-permute-start(f32[4,128,128]{2,1,0:T(8,128)} %bitcast.9), channel_id=1, source_target_pairs={{0,1},{1,0},{2,3},{3,2},{4,5},{5,4},{6,7},{7,6},{8,9},{9,8},{10,11... | collective-permute-start | bytes 786440 | tf_op jit(solution)/shard_map/ppermute | solution.py:155
  20.6 6.9 %collective-permute-start.10 = (f32[4,128,128]{2,1,0:T(8,128)S(1)}, f32[4,128,128]{2,1,0:T(8,128)S(1)}, u32[]{:S(2)}, u32[]{:S(2)}) collective-permute-start(f32[4,128,128]{2,1,0:T(8,128)S(1)} %collective-permute-done.8.refs_12_.refs_16_.refs_8_), channel_id=1, source_target_pairs={{0,16},{16,0},{1,17},{17,1},{2,18},{18,2},{3,19},{19,3},{4,20},{20... | collective-permute-start | bytes 786440 | tf_op jit(solution)/shard_map/ppermute | solution.py:158
  21.8 8.3 %collective-permute-start.9 = (f32[4,128,128]{2,1,0:T(8,128)S(1)}, f32[4,128,128]{2,1,0:T(8,128)S(1)}, u32[]{:S(2)}, u32[]{:S(2)}) collective-permute-start(f32[4,128,128]{2,1,0:T(8,128)S(1)} %collective-permute-done.8.refs_12_.refs_16_.refs_8_), channel_id=1, source_target_pairs={{0,1},{1,0},{2,3},{3,2},{4,5},{5,4},{6,7},{7,6},{8,9},{9,8},{10,11... | collective-permute-start | bytes 786440 | tf_op jit(solution)/shard_map/ppermute | solution.py:155
  25.3 13.7 %collective-permute-start.16 = (f32[8,128,128]{2,1,0:T(8,128)}, f32[8,128,128]{2,1,0:T(8,128)S(1)}, u32[]{:S(2)}, u32[]{:S(2)}) collective-permute-start(f32[8,128,128]{2,1,0:T(8,128)} %bitcast.15), channel_id=1, source_target_pairs={{0,2},{1,3},{2,0},{3,1},{4,6},{5,7},{6,4},{7,5},{8,10},{9,11},{10,... | collective-permute-start | bytes 1572872 | tf_op jit(solution)/shard_map/ppermute | solution.py:155
  26.0 16.7 %collective-permute-start.2 = (f32[8,128,128]{2,1,0:T(8,128)S(1)}, f32[8,128,128]{2,1,0:T(8,128)}, u32[]{:S(2)}, u32[]{:S(2)}) collective-permute-start(f32[8,128,128]{2,1,0:T(8,128)S(1)} %collective-permute-done.1), channel_id=1, source_target_pairs={{0,4},{4,0},{8,12},{12,8},{1,5},{5,1},{9,13},{13,9},{2,6},{6,2},{1... | collective-permute-start | bytes 1572872 | tf_op jit(solution)/shard_map/ppermute | solution.py:161
  26.4 42.8 %copy-start.20 = (s32[1,1,1,2,4,3,16]{6,4,5,3,2,1,0:T(4,128)S(1)}, s32[1,1,1,2,4,3,16]{6,4,5,3,2,1,0:T(4,128)}, u32[]{:S(2)}) copy-start(s32[1,1,1,2,4,3,16]{6,4,5,3,2,1,0:T(4,128)} %param.6) | copy-start | bytes 4612
  27.5 46.6 %copy-start.3 = (f32[4,128,128]{2,1,0:T(8,128)}, f32[4,128,128]{2,1,0:T(8,128)S(1)}, u32[]{:S(2)}) copy-start(f32[4,128,128]{2,1,0:T(8,128)S(1)} %collective-permute-done.10.refs_14_.refs_18_.refs_10_) | copy-start | bytes 786436
  27.5 17.0 %collective-permute-start.23 = (f32[8,128,128]{2,1,0:T(8,128)}, f32[8,128,128]{2,1,0:T(8,128)S(1)}, u32[]{:S(2)}, u32[]{:S(2)}) collective-permute-start(f32[8,128,128]{2,1,0:T(8,128)} %bitcast.16), channel_id=1, source_target_pairs={{0,1},{1,0},{2,3},{3,2},{4,5},{5,4},{6,7},{7,6},{8,9},{9,8},{10,11... | collective-permute-start | bytes 1572872 | tf_op jit(solution)/shard_map/ppermute | solution.py:155
  30.1 43.9 %copy-start.4 = (f32[4,128,128]{2,1,0:T(8,128)}, f32[4,128,128]{2,1,0:T(8,128)S(1)}, u32[]{:S(2)}) copy-start(f32[4,128,128]{2,1,0:T(8,128)S(1)} %collective-permute-done.9.refs_13_.refs_17_.refs_9_) | copy-start | bytes 786436
  30.1 2.1 %collective-permute-start.7 = (f32[4,128,128]{2,1,0:T(8,128)S(1)}, f32[4,128,128]{2,1,0:T(8,128)S(1)}, u32[]{:S(2)}, u32[]{:S(2)}) collective-permute-start(f32[4,128,128]{2,1,0:T(8,128)S(1)} %collective-permute-done.6.refs_10_.refs_14_.refs_6_), channel_id=1, source_target_pairs={{0,1},{1,0},{2,3},{3,2},{4,5},{5,4},{6,7},{7,6},{8,9},{9,8},{10,11... | collective-permute-start | bytes 786440 | tf_op jit(solution)/shard_map/ppermute | solution.py:155
  30.2 11.6 %collective-permute-start.18 = (f32[2,128,128]{2,1,0:T(8,128)S(1)}, f32[2,128,128]{2,1,0:T(8,128)S(1)}, u32[]{:S(2)}, u32[]{:S(2)}) collective-permute-start(f32[2,128,128]{2,1,0:T(8,128)S(1)} %slice.9), channel_id=1, source_target_pairs={{0,2},{1,3},{2,0},{3,1},{4,6},{5,7},{6,4},{7,5},{8,10},{9,11},{10,... | collective-permute-start | bytes 393224 | tf_op jit(solution)/shard_map/ppermute | solution.py:155
  32.1 48.5 %copy-start.7 = (f32[8,128,128]{2,1,0:T(8,128)}, f32[8,128,128]{2,1,0:T(8,128)S(1)}, u32[]{:S(2)}) copy-start(f32[8,128,128]{2,1,0:T(8,128)S(1)} %broadcast_select_fusion.refs_2_) | copy-start | bytes 1572868
  32.2 41.8 %copy-start.5 = (f32[4,128,128]{2,1,0:T(8,128)}, f32[4,128,128]{2,1,0:T(8,128)S(1)}, u32[]{:S(2)}) copy-start(f32[4,128,128]{2,1,0:T(8,128)S(1)} %collective-permute-done.7.refs_11_.refs_15_.refs_7_) | copy-start | bytes 786436
  32.2 13.2 %collective-permute-start.11 = (f32[4,128,128]{2,1,0:T(8,128)S(1)}, f32[4,128,128]{2,1,0:T(8,128)S(1)}, u32[]{:S(2)}, u32[]{:S(2)}) collective-permute-start(f32[4,128,128]{2,1,0:T(8,128)S(1)} %collective-permute-done.10.refs_14_.refs_18_.refs_10_), channel_id=1, source_target_pairs={{0,1},{1,0},{2,3},{3,2},{4,5},{5,4},{6,7},{7,6},{8,9},{9,8},{10,11... | collective-permute-start | bytes 786440 | tf_op jit(solution)/shard_map/ppermute | solution.py:155
  39.0 18.6 %collective-permute-start.25 = (f32[8,128,128]{2,1,0:T(8,128)S(1)}, f32[8,128,128]{2,1,0:T(8,128)S(1)}, u32[]{:S(2)}, u32[]{:S(2)}) collective-permute-start(f32[8,128,128]{2,1,0:T(8,128)S(1)} %collective-permute-done.16.refs_6_), channel_id=1, source_target_pairs={{0,1},{1,0},{2,3},{3,2},{4,5},{5,4},{6,7},{7,6},{8,9},{9,8},{10,11... | collective-permute-start | bytes 1572872 | tf_op jit(solution)/shard_map/ppermute | solution.py:155
  41.8 38.9 %copy-start.18 = (f32[2,128,128]{2,1,0:T(8,128)}, f32[2,128,128]{2,1,0:T(8,128)S(1)}, u32[]{:S(2)}) copy-start(f32[2,128,128]{2,1,0:T(8,128)S(1)} %collective-permute-done.18.refs_7_) | copy-start | bytes 393220
  41.8 3.7 %collective-permute-start.20 = (f32[2,128,128]{2,1,0:T(8,128)S(1)}, f32[2,128,128]{2,1,0:T(8,128)S(1)}, u32[]{:S(2)}, u32[]{:S(2)}) collective-permute-start(f32[2,128,128]{2,1,0:T(8,128)S(1)} %collective-permute-done.18.refs_7_), channel_id=1, source_target_pairs={{0,1},{1,0},{2,3},{3,2},{4,5},{5,4},{6,7},{7,6},{8,9},{9,8},{10,11... | collective-permute-start | bytes 393224 | tf_op jit(solution)/shard_map/ppermute | solution.py:155
  42.7 14.5 %collective-permute-start.21 = (f32[8,128,128]{2,1,0:T(8,128)S(1)}, f32[8,128,128]{2,1,0:T(8,128)}, u32[]{:S(2)}, u32[]{:S(2)}) collective-permute-start(f32[8,128,128]{2,1,0:T(8,128)S(1)} %broadcast_select_fusion.refs_2_), channel_id=1, source_target_pairs={{0,2},{1,3},{2,0},{3,1},{4,6},{5,7},{6,4},{7,5},{8,10},{9,11},{10,... | collective-permute-start | bytes 1572872 | tf_op jit(solution)/shard_map/ppermute | solution.py:155
  44.5 22.9 %collective-permute-start.3 = (f32[8,128,128]{2,1,0:T(8,128)S(1)}, f32[8,128,128]{2,1,0:T(8,128)}, u32[]{:S(2)}, u32[]{:S(2)}) collective-permute-start(f32[8,128,128]{2,1,0:T(8,128)S(1)} %broadcast_select_fusion.1.refs_4_), channel_id=1, source_target_pairs={{0,2},{1,3},{2,0},{3,1},{4,6},{5,7},{6,4},{7,5},{8,10},{9,11},{10,... | collective-permute-start | bytes 1572872 | tf_op jit(solution)/shard_map/ppermute | solution.py:155
  45.4 10.2 %collective-permute-start.17 = (f32[6,128,128]{2,1,0:T(8,128)S(1)}, f32[6,128,128]{2,1,0:T(8,128)}, u32[]{:S(2)}, u32[]{:S(2)}) collective-permute-start(f32[6,128,128]{2,1,0:T(8,128)S(1)} %slice.8), channel_id=1, source_target_pairs={{0,4},{4,0},{8,12},{12,8},{1,5},{5,1},{9,13},{13,9},{2,6},{6,2},{1... | collective-permute-start | bytes 1179656 | tf_op jit(solution)/shard_map/ppermute | solution.py:161
  45.5 22.8 %collective-permute-start.24 = (f32[8,128,128]{2,1,0:T(8,128)S(1)}, f32[8,128,128]{2,1,0:T(8,128)S(1)}, u32[]{:S(2)}, u32[]{:S(2)}) collective-permute-start(f32[8,128,128]{2,1,0:T(8,128)S(1)} %copy-done.11), channel_id=1, source_target_pairs={{0,1},{1,0},{2,3},{3,2},{4,5},{5,4},{6,7},{7,6},{8,9},{9,8},{10,11... | collective-permute-start | bytes 1572872 | tf_op jit(solution)/shard_map/ppermute | solution.py:155
  55.6 25.1 %collective-permute-start.14 = (f32[8,128,128]{2,1,0:T(8,128)S(1)}, f32[8,128,128]{2,1,0:T(8,128)S(1)}, u32[]{:S(2)}, u32[]{:S(2)}) collective-permute-start(f32[8,128,128]{2,1,0:T(8,128)S(1)} %broadcast_select_fusion.refs_2_), channel_id=1, source_target_pairs={{0,1},{1,0},{2,3},{3,2},{4,5},{5,4},{6,7},{7,6},{8,9},{9,8},{10,11... | collective-permute-start | bytes 1572872 | tf_op jit(solution)/shard_map/ppermute | solution.py:155
  57.1 23.6 %collective-permute-start.22 = (f32[8,128,128]{2,1,0:T(8,128)}, f32[8,128,128]{2,1,0:T(8,128)}, u32[]{:S(2)}, u32[]{:S(2)}) collective-permute-start(f32[8,128,128]{2,1,0:T(8,128)} %collective-permute-done.21.refs_10_), channel_id=1, source_target_pairs={{0,1},{1,0},{2,3},{3,2},{4,5},{5,4},{6,7},{7,6},{8,9},{9,8},{10,11... | collective-permute-start | bytes 1572872 | tf_op jit(solution)/shard_map/ppermute | solution.py:155
  57.6 23.1 %collective-permute-start.15 = (f32[8,128,128]{2,1,0:T(8,128)S(1)}, f32[8,128,128]{2,1,0:T(8,128)}, u32[]{:S(2)}, u32[]{:S(2)}) collective-permute-start(f32[8,128,128]{2,1,0:T(8,128)S(1)} %broadcast_select_fusion.1.refs_4_), channel_id=1, source_target_pairs={{0,1},{1,0},{2,3},{3,2},{4,5},{5,4},{6,7},{7,6},{8,9},{9,8},{10,11... | collective-permute-start | bytes 1572872 | tf_op jit(solution)/shard_map/ppermute | solution.py:155
  67.4 22.2 %collective-permute-start.4 = (f32[8,128,128]{2,1,0:T(8,128)}, f32[8,128,128]{2,1,0:T(8,128)}, u32[]{:S(2)}, u32[]{:S(2)}) collective-permute-start(f32[8,128,128]{2,1,0:T(8,128)} %collective-permute-done.3.refs_2_), channel_id=1, source_target_pairs={{0,1},{1,0},{2,3},{3,2},{4,5},{5,4},{6,7},{7,6},{8,9},{9,8},{10,11... | collective-permute-start | bytes 1572872 | tf_op jit(solution)/shard_map/ppermute | solution.py:155
  69.2 11.5 %collective-permute-start.19 = (f32[6,128,128]{2,1,0:T(8,128)}, f32[6,128,128]{2,1,0:T(8,128)}, u32[]{:S(2)}, u32[]{:S(2)}) collective-permute-start(f32[6,128,128]{2,1,0:T(8,128)} %collective-permute-done.17.refs_6_), channel_id=1, source_target_pairs={{0,1},{1,0},{2,3},{3,2},{4,5},{5,4},{6,7},{7,6},{8,9},{9,8},{10,11... | collective-permute-start | bytes 1179656 | tf_op jit(solution)/shard_map/ppermute | solution.py:155
  (15 other events, 292.3 us)

commit v2 on v1

--- a/solution.py
+++ b/solution.py
@@ -7,30 +7,32 @@
 from jax.experimental.pallas import tpu as pltpu
 from jax.sharding import PartitionSpec as P
 
+
 CL = 32
 UNROLL = 8
+VMEM_LIMIT = 20 << 20
 F32 = jnp.float32
 BF16 = jnp.bfloat16
 
 
-def sort_kernel(rel_of, stage_of, base_of, a_cap, b_of, plan, counts, lists, sizes, stage_tab, base_tab):
+def sort_kernel(rel_of, place_of, a_cap, cut, b_of, plan, counts, lists, sizes, stage_tab, base_tab):
     shards, layers, _, _ = plan.shape
-    n_col = stage_tab.shape[0] // layers
+    n_col = stage_tab.shape[0] // (2 * layers)
     stages = sizes.shape[0]
-    room = lists.shape[1]
     z, me = lax.axis_index("col"), lax.axis_index("layer")
     row = lax.axis_index("row")
-    rels = sorted({rel for rel, _ in stage_of})
+    rels = sorted({rel for rel, _, _ in place_of})
     for zp in range(n_col):
         rel = rel_of(zp, z)
         for dm in range(layers):
-            stage = jnp.int32(0)
-            base = jnp.int32(0)
-            for r in rels:
-                stage = jnp.where(rel == r, stage_of[r, dm], stage)
-                base = jnp.where(rel == r, base_of[r, dm], base)
-            stage_tab[zp * layers + dm] = stage
-            base_tab[zp * layers + dm] = base
+            for part in (0, 1):
+                stage = jnp.int32(0)
+                base = jnp.int32(0)
+                for r in rels:
+                    stage = jnp.where(rel == r, place_of[r, dm, part][0], stage)
+                    base = jnp.where(rel == r, place_of[r, dm, part][1], base)
+                stage_tab[(zp * layers + dm) * 2 + part] = stage
+                base_tab[(zp * layers + dm) * 2 + part] = base
     for st in range(stages):
         sizes[st] = 0
 
@@ -41,11 +43,12 @@
 
         def per_pair(p, _):
             left = plan[s, m, 0, p]
-            at = (left // (layers * a_cap)) * layers + dm
+            within = left % a_cap
+            at = ((left // (layers * a_cap)) * layers + dm) * 2 + jnp.where(within >= cut, 1, 0)
             st = stage_tab[at]
             pos = sizes[st]
             lists[st, pos] = (
-                (base_tab[at] + left % a_cap) | ((b_base + plan[s, m, 1, p]) << 10) | (plan[s, m, 2, p] << 20)
+                (base_tab[at] + within) | ((b_base + plan[s, m, 1, p]) << 10) | (plan[s, m, 2, p] << 20)
             )
             sizes[st] = pos + 1
             return 0
@@ -57,7 +60,6 @@
         n = sizes[st]
         for u in range(UNROLL - 1):
             lists[st, n + u] = CL << 20
-    del room
 
 
 def halves(x):
@@ -139,11 +141,11 @@
         cost_estimate=pl.CostEstimate(
             flops=6 * pairs * bs[0] * bs[0] * bs[1], bytes_accessed=4 * bs[0] * bs[1] * 80, transcendentals=0
         ),
-        name=f"stage_{stage}",
+        compiler_params=pltpu.CompilerParams(vmem_limit_bytes=VMEM_LIMIT),
     )(sizes, lists, *arrays)
 
 
-def per_device(a_blocks, b_blocks, pair_plan, pair_counts):
+def multiply(a_blocks, b_blocks, pair_plan, pair_counts):
     n_row, n_col, n_layer = (lax.axis_size(x) for x in ("row", "col", "layer"))
     z = lax.axis_index("col")
     own, b_own = a_blocks[0], b_blocks[:, 0]
@@ -151,8 +153,11 @@
     plan, counts = pair_plan[0, 0, 0], pair_counts[0, 0, 0]
     half = n_layer // 2
 
-    def over_layer(x, d):
+    def over_layer(x, d=half):
         return lax.ppermute(x, "layer", [(i, i ^ d) for i in range(n_layer)])
+
+    def core(x):
+        return over_layer(x, 1)
 
     def over_row(x):
         return lax.ppermute(x, "row", [(i, i ^ 1) for i in range(n_row)])
@@ -170,45 +175,56 @@
         return lax.ppermute(x, ("col", "layer"), moves)
 
     is_end = jnp.logical_or(z == 0, z == n_col - 1)
-    g = a_cap * 3 // 4
-    y_own = over_layer(own, half)
+    g = a_cap // 2
+    y_own = over_layer(own)
     p_a = pairs_end(own)
     p_b = pairs_mid(own)
-    y_b = over_layer(b_own, half)
-    x_b = over_row(b_own)
+    swapped = n_row == 2
+    b_here = b_own if swapped else lax.all_gather(b_own, "row", axis=0, tiled=True)
+    y_b = over_layer(b_here)
+    if swapped:
+        x_b = over_row(b_own)
+        b_rows = dict(b=b_own, xb=x_b, yb=y_b, xyb=over_row(y_b))
+    else:
+        b_rows = dict(b=b_here, yb=y_b)
     q = pairs_mid(p_a)
     r = pairs_end(p_b)
-    y_a = over_layer(p_a[g:], half)
+    y_a = over_layer(p_a[g:])
     x2 = jnp.where(is_end, r, p_b)
-    y_2 = over_layer(x2, half)
-    x_yb = over_row(y_b)
+    y_2 = over_layer(x2)
     t = pairs_end(q)
     x3 = jnp.where(is_end, t, q)
-    y_3 = over_layer(x3, half)
+    y_3 = over_layer(x3)
     p_y = pairs_end(y_own[:g])
+    c_of = {}
+    for name, x in dict(own=own, pa=p_a, yown=y_own, x2=x2, x3=x3, ya=y_a, y2=y_2, py=p_y, y3=y_3).items():
+        c_of[name] = (x, core(x))
 
     stages = [
-        [((0, 0), [own]), ((1, 0), [p_a]), ((0, half), [y_own])],
-        [((2, 0), [x2]), ((3, 0), [x3]), ((1, half), [p_y, y_a]), ((2, half), [y_2])],
-        [((3, half), [y_3])],
+        [(0, 0, (0, 1), "own"), (1, 0, (0, 1), "pa"), (0, half, (0, 1), "yown")],
+        [(2, 0, (0, 1), "x2"), (3, 0, (0, 1), "x3"), (1, half, (1,), "ya"), (2, half, (0, 1), "y2")],
+        [(3, half, (0, 1), "y3"), (1, half, (0,), "py")],
     ]
-    stage_of, base_of, a_parts = {}, {}, []
+    place_of, a_parts = {}, []
     for st, groups in enumerate(stages):
         at, parts = 0, []
-        for (rel, dm), arrays in groups:
+        for rel, dm, halves_here, name in groups:
             for other in (0, 1):
-                stage_of[rel, dm ^ other], base_of[rel, dm ^ other] = st, at
-                for x in arrays:
-                    parts.append((over_layer(x, 1) if other else x, at, x.shape[0]))
-                    at += x.shape[0]
+                x = c_of[name][other]
+                for part in halves_here:
+                    place_of[rel, dm ^ other, part] = (st, at - (g if halves_here == (1,) else 0))
+                parts.append((x, at, x.shape[0]))
+                at += x.shape[0]
         a_parts.append(parts)
 
     b_parts = []
-    for x in (b_own, x_b, y_b, x_yb):
-        b_parts += [x, over_layer(x, 1)]
+    for x in b_rows.values():
+        b_parts += [x, core(x)]
 
     def b_of(s, row, dm):
-        return ((dm // half) * 4 + (s ^ row) * 2 + dm % half) * b_cap
+        within = 0 if swapped else s * b_cap
+        place = s ^ row if swapped else 0
+        return ((dm // half) * len(b_rows) + place * 2 + dm % half) * b_parts[0].shape[0] + within
 
     def rel_of(zp, z):
         far = jnp.int32(3 if zp in (0, n_col - 1) else 2)
@@ -218,15 +234,16 @@
     room = shards * layers * p_cap + UNROLL
     smem = pl.BlockSpec(memory_space=pltpu.SMEM)
     lists, sizes = pl.pallas_call(
-        functools.partial(sort_kernel, rel_of, stage_of, base_of, a_cap, b_of),
+        functools.partial(sort_kernel, rel_of, place_of, a_cap, g, b_of),
         out_shape=(
             jax.ShapeDtypeStruct((len(stages), room), jnp.int32),
             jax.ShapeDtypeStruct((len(stages),), jnp.int32),
         ),
         in_specs=[smem, smem],
         out_specs=(smem, smem),
-        scratch_shapes=[pltpu.SMEM((n_col * layers,), jnp.int32), pltpu.SMEM((n_col * layers,), jnp.int32)],
-        name="sort_pairs",
+        scratch_shapes=[pltpu.SMEM((n_col * layers * 2,), jnp.int32)] * 2,
+        cost_estimate=pl.CostEstimate(flops=0, bytes_accessed=4000, transcendentals=0),
+        name="sort",
     )(plan, counts)
     acc = None
     for st, parts in enumerate(a_parts):
@@ -242,6 +259,4 @@
         P("row", "col", "layer", None, None),
     )
     out_specs = P("row", "col", "layer", None, None)
-    return jax.shard_map(
-        per_device, mesh=mesh, in_specs=in_specs, out_specs=out_specs, check_vma=False
-    )
+    return jax.shard_map(multiply, mesh=mesh, in_specs=in_specs, out_specs=out_specs, check_vma=False)

time: 95.7 us -> 97.6 us (1.020)
  the two profiles are of different devices: /device:TPU:9 before, /device:TPU:1 now
where the time goes in v2:
time: 97.6 us; the launch traced here: 97 us
  starting transfers between devices  35.1 us (36%)
  waiting for transfers between devices  29.6 us (30%)
  Pallas kernels  18.6 us (19%)
  local copies, waits for them, and re-layouts  11.3 us (12%)
  other arithmetic  2.2 us (2%)
    ppermute x18, starting transfers between devices, over_layer(): return lax.ppermute(x, 'layer', [(i, i ^ d) for i in range(n_layer)])  21.2 us
    pallas_call x3, Pallas kernels, run_stage(): pl.pallas_call(functools.partial(stage_kernel, stage, [(at, n) for _, at,...  13.7 us
    ppermute x18, waiting for transfers between devices, over_layer(): return lax.ppermute(x, 'layer', [(i, i ^ d) for i in range(n_layer)])  13.2 us
    ppermute x4, waiting for transfers between devices, pairs_end(): return lax.ppermute(x, 'col', [(i, i ^ 1) for i in range(n_col)])  11.3 us
    unnamed x35, local copies, waits for them, and re-layouts  10.2 us
    ppermute x4, starting transfers between devices, pairs_end(): return lax.ppermute(x, 'col', [(i, i ^ 1) for i in range(n_col)])  9.31 us
    ppermute x2, waiting for transfers between devices, over_row(): return lax.ppermute(x, 'row', [(i, i ^ 1) for i in range(n_row)])  5.1 us
    pallas_call x1, Pallas kernels, multiply(): pl.pallas_call(functools.partial(sort_kernel, rel_of, place_of, a_cap, g,...  4.91 us
  transfers between devices with their start and end apart: 26, of which 6 were waited for; matrix products, arithmetic and copies ran while one was open for 4% of the time, Pallas kernels for 15%

profile of v2, /device:TPU:1, one launch (start us, length us, event | category | flops | bytes accessed | tf_op | source)
XLA Modules:
  0.0 97.0 jit_solution(6077469210627645443)
XLA Ops:
  0.0 2.1 %collective-permute-start = (f32[8,128,128]{2,1,0:T(8,128)}, f32[8,128,128]{2,1,0:T(8,128)S(1)}, u32[]{:S(2)}, u32[]{:S(2)}) collective-permute-start(f32[8,128,128]{2,1,0:T(8,128)} %bitcast.13), channel_id=1, source_target_pairs={{0,4},{4,0},{8,12},{12,8},{1,5},{5,1},{9,13},{13,9},{2,6},{6,2},{1... | collective-permute-start | bytes 1572872 | tf_op jit(solution)/shard_map/ppermute | solution.py:166
  3.1 1.2 %collective-permute-start.5 = (f32[8,128,128]{2,1,0:T(8,128)}, f32[8,128,128]{2,1,0:T(8,128)}, u32[]{:S(2)}, u32[]{:S(2)}) collective-permute-start(f32[8,128,128]{2,1,0:T(8,128)} %bitcast.15), channel_id=1, source_target_pairs={{0,2},{1,3},{2,0},{3,1},{4,6},{5,7},{6,4},{7,5},{8,10},{9,11},{10,... | collective-permute-start | bytes 1572872 | tf_op jit(solution)/shard_map/ppermute | solution.py:157
  4.3 9.7 %collective-permute-done.refs_4_ = f32[8,128,128]{2,1,0:T(8,128)S(1)} collective-permute-done((f32[8,128,128]{2,1,0:T(8,128)}, f32[8,128,128]{2,1,0:T(8,128)S(1)}, u32[]{:S(2)}, u32[]{:S(2)}) %collective-permute-start) | collective-permute-done | bytes 524320 | tf_op jit(solution)/shard_map/ppermute | solution.py:166
  14.1 1.1 %collective-permute-start.1 = (f32[8,128,128]{2,1,0:T(8,128)S(1)}, f32[8,128,128]{2,1,0:T(8,128)S(1)}, u32[]{:S(2)}, u32[]{:S(2)}) collective-permute-start(f32[8,128,128]{2,1,0:T(8,128)S(1)} %collective-permute-done.refs_4_), channel_id=1, source_target_pairs={{0,1},{1,0},{2,3},{3,2},{4,8},{5,9},{6,10},{7,11},{8,4},{9,5},{10,... | collective-permute-start | bytes 1572872 | tf_op jit(solution)/shard_map/ppermute | solution.py:175
  15.2 1.3 %collective-permute-start.16 = (f32[8,128,128]{2,1,0:T(8,128)S(1)}, f32[8,128,128]{2,1,0:T(8,128)}, u32[]{:S(2)}, u32[]{:S(2)}) collective-permute-start(f32[8,128,128]{2,1,0:T(8,128)S(1)} %collective-permute-done.15), channel_id=1, source_target_pairs={{0,4},{4,0},{8,12},{12,8},{1,5},{5,1},{9,13},{13,9},{2,6},{6,2},{1... | collective-permute-start | bytes 1572872 | tf_op jit(solution)/shard_map/ppermute | solution.py:166
  16.5 1.2 %collective-permute-start.11 = (f32[4,128,128]{2,1,0:T(8,128)}, f32[4,128,128]{2,1,0:T(8,128)S(1)}, u32[]{:S(2)}, u32[]{:S(2)}) collective-permute-start(f32[4,128,128]{2,1,0:T(8,128)} %bitcast.7), channel_id=1, source_target_pairs={{0,2},{1,3},{2,0},{3,1},{4,6},{5,7},{6,4},{7,5},{8,10},{9,11},{10,... | collective-permute-start | bytes 786440 | tf_op jit(solution)/shard_map/ppermute | solution.py:157
  17.8 1.2 %collective-permute-start.9 = (f32[4,128,128]{2,1,0:T(8,128)}, f32[4,128,128]{2,1,0:T(8,128)S(1)}, u32[]{:S(2)}, u32[]{:S(2)}) collective-permute-start(f32[4,128,128]{2,1,0:T(8,128)} %bitcast.8), channel_id=1, source_target_pairs={{0,16},{16,0},{1,17},{17,1},{2,18},{18,2},{3,19},{19,3},{4,20},{20... | collective-permute-start | bytes 786440 | tf_op jit(solution)/shard_map/ppermute | solution.py:163
  19.0 2.5 %collective-permute-start.8 = (f32[4,128,128]{2,1,0:T(8,128)}, f32[4,128,128]{2,1,0:T(8,128)S(1)}, u32[]{:S(2)}, u32[]{:S(2)}) collective-permute-start(f32[4,128,128]{2,1,0:T(8,128)} %bitcast.9), channel_id=1, source_target_pairs={{0,1},{1,0},{2,3},{3,2},{4,5},{5,4},{6,7},{7,6},{8,9},{9,8},{10,11... | collective-permute-start | bytes 786440 | tf_op jit(solution)/shard_map/ppermute | solution.py:157
  21.5 5.9 %collective-permute-start.2 = (f32[8,128,128]{2,1,0:T(8,128)S(1)}, f32[8,128,128]{2,1,0:T(8,128)}, u32[]{:S(2)}, u32[]{:S(2)}) collective-permute-start(f32[8,128,128]{2,1,0:T(8,128)S(1)} %collective-permute-done.1), channel_id=1, source_target_pairs={{0,4},{4,0},{8,12},{12,8},{1,5},{5,1},{9,13},{13,9},{2,6},{6,2},{1... | collective-permute-start | bytes 1572872 | tf_op jit(solution)/shard_map/ppermute | solution.py:166
  28.5 2.5 %collective-permute-start.23 = (f32[8,128,128]{2,1,0:T(8,128)}, f32[8,128,128]{2,1,0:T(8,128)S(1)}, u32[]{:S(2)}, u32[]{:S(2)}) collective-permute-start(f32[8,128,128]{2,1,0:T(8,128)} %bitcast.16), channel_id=1, source_target_pairs={{0,1},{1,0},{2,3},{3,2},{4,5},{5,4},{6,7},{7,6},{8,9},{9,8},{10,11... | collective-permute-start | bytes 1572872 | tf_op jit(solution)/shard_map/ppermute | solution.py:157
  31.0 1.3 %collective-permute-start.13 = (f32[4,128,128]{2,1,0:T(8,128)S(1)}, f32[4,128,128]{2,1,0:T(8,128)S(1)}, u32[]{:S(2)}, u32[]{:S(2)}) collective-permute-start(f32[4,128,128]{2,1,0:T(8,128)S(1)} %collective-permute-done.11.refs_12_.refs_14_.refs_10_), channel_id=1, source_target_pairs={{0,16},{16,0},{1,17},{17,1},{2,18},{18,2},{3,19},{19,3},{4,20},{20... | collective-permute-start | bytes 786440 | tf_op jit(solution)/shard_map/ppermute | solution.py:163
  32.8 1.1 %broadcast_select_fusion.refs_2_ = f32[8,128,128]{2,1,0:T(8,128)S(1)} fusion(f32[8,128,128]{2,1,0:T(8,128)} %collective-permute-done.16, f32[8,128,128]{2,1,0:T(8,128)S(1)} %collective-permute-done.15, pred[]{:T(512)S(6)} %or.3), kind=kLoop, calls=%fused_computation | loop fusion | flops 131072 | bytes 1572865 | tf_op jit(solution)/shard_map/jit(_where)/select_n | solution.py:193
  33.9 5.1 %collective-permute-done.13.refs_14_.refs_16_.refs_12_ = f32[4,128,128]{2,1,0:T(8,128)S(1)} collective-permute-done((f32[4,128,128]{2,1,0:T(8,128)S(1)}, f32[4,128,128]{2,1,0:T(8,128)S(1)}, u32[]{:S(2)}, u32[]{:S(2)}) %collective-permute-start.13) | collective-permute-done | bytes 262176 | tf_op jit(solution)/shard_map/ppermute | solution.py:163
  39.0 1.2 %collective-permute-start.19 = (f32[4,128,128]{2,1,0:T(8,128)S(1)}, f32[4,128,128]{2,1,0:T(8,128)S(1)}, u32[]{:S(2)}, u32[]{:S(2)}) collective-permute-start(f32[4,128,128]{2,1,0:T(8,128)S(1)} %slice.9), channel_id=1, source_target_pairs={{0,2},{1,3},{2,0},{3,1},{4,6},{5,7},{6,4},{7,5},{8,10},{9,11},{10,... | collective-permute-start | bytes 786440 | tf_op jit(solution)/shard_map/ppermute | solution.py:157
  40.2 1.1 %collective-permute-start.25 = (f32[8,128,128]{2,1,0:T(8,128)}, f32[8,128,128]{2,1,0:T(8,128)S(1)}, u32[]{:S(2)}, u32[]{:S(2)}) collective-permute-start(f32[8,128,128]{2,1,0:T(8,128)} %collective-permute-done.5.refs_6_), channel_id=1, source_target_pairs={{0,1},{1,0},{2,3},{3,2},{4,5},{5,4},{6,7},{7,6},{8,9},{9,8},{10,11... | collective-permute-start | bytes 1572872 | tf_op jit(solution)/shard_map/ppermute | solution.py:157
  41.6 1.1 %broadcast_select_fusion.1.refs_4_ = f32[8,128,128]{2,1,0:T(8,128)S(1)} fusion(f32[8,128,128]{2,1,0:T(8,128)} %collective-permute-done.2, f32[8,128,128]{2,1,0:T(8,128)} %copy-done.15, pred[]{:T(512)S(6)} %or.3), kind=kLoop, calls=%fused_computation.1 | loop fusion | flops 131072 | bytes 1572865 | tf_op jit(solution)/shard_map/jit(_where)/select_n | solution.py:196
  43.5 1.2 %collective-permute-start.3 = (f32[8,128,128]{2,1,0:T(8,128)S(1)}, f32[8,128,128]{2,1,0:T(8,128)}, u32[]{:S(2)}, u32[]{:S(2)}) collective-permute-start(f32[8,128,128]{2,1,0:T(8,128)S(1)} %broadcast_select_fusion.1.refs_4_), channel_id=1, source_target_pairs={{0,2},{1,3},{2,0},{3,1},{4,6},{5,7},{6,4},{7,5},{8,10},{9,11},{10,... | collective-permute-start | bytes 1572872 | tf_op jit(solution)/shard_map/ppermute | solution.py:157
  44.8 1.3 %collective-permute-done.19.refs_6_ = f32[4,128,128]{2,1,0:T(8,128)S(1)} collective-permute-done((f32[4,128,128]{2,1,0:T(8,128)S(1)}, f32[4,128,128]{2,1,0:T(8,128)S(1)}, u32[]{:S(2)}, u32[]{:S(2)}) %collective-permute-start.19) | collective-permute-done | bytes 262176 | tf_op jit(solution)/shard_map/ppermute | solution.py:157
  46.0 2.9 %collective-permute-start.20 = (f32[4,128,128]{2,1,0:T(8,128)S(1)}, f32[4,128,128]{2,1,0:T(8,128)S(1)}, u32[]{:S(2)}, u32[]{:S(2)}) collective-permute-start(f32[4,128,128]{2,1,0:T(8,128)S(1)} %collective-permute-done.19.refs_6_), channel_id=1, source_target_pairs={{0,1},{1,0},{2,3},{3,2},{4,5},{5,4},{6,7},{7,6},{8,9},{9,8},{10,11... | collective-permute-start | bytes 786440 | tf_op jit(solution)/shard_map/ppermute | solution.py:157
  48.9 1.6 %collective-permute-done.6.refs_4_ = f32[4,128,128]{2,1,0:T(8,128)} collective-permute-done((f32[4,128,128]{2,1,0:T(8,128)S(1)}, f32[4,128,128]{2,1,0:T(8,128)}, u32[]{:S(2)}, u32[]{:S(2)}) %collective-permute-start.6) | collective-permute-done | bytes 262176 | tf_op jit(solution)/shard_map/ppermute | solution.py:166
  50.5 1.8 %collective-permute-start.24 = (f32[8,128,128]{2,1,0:T(8,128)S(1)}, f32[8,128,128]{2,1,0:T(8,128)S(1)}, u32[]{:S(2)}, u32[]{:S(2)}) collective-permute-start(f32[8,128,128]{2,1,0:T(8,128)S(1)} %copy-done.2), channel_id=1, source_target_pairs={{0,1},{1,0},{2,3},{3,2},{4,5},{5,4},{6,7},{7,6},{8,9},{9,8},{10,11... | collective-permute-start | bytes 1572872 | tf_op jit(solution)/shard_map/ppermute | solution.py:157
  53.2 4.2 %collective-permute-done.21.refs_8_ = f32[8,128,128]{2,1,0:T(8,128)} collective-permute-done((f32[8,128,128]{2,1,0:T(8,128)S(1)}, f32[8,128,128]{2,1,0:T(8,128)}, u32[]{:S(2)}, u32[]{:S(2)}) %collective-permute-start.21) | collective-permute-done | bytes 524320 | tf_op jit(solution)/shard_map/ppermute | solution.py:157
  57.4 2.9 %collective-permute-start.22 = (f32[8,128,128]{2,1,0:T(8,128)}, f32[8,128,128]{2,1,0:T(8,128)}, u32[]{:S(2)}, u32[]{:S(2)}) collective-permute-start(f32[8,128,128]{2,1,0:T(8,128)} %collective-permute-done.21.refs_8_), channel_id=1, source_target_pairs={{0,1},{1,0},{2,3},{3,2},{4,5},{5,4},{6,7},{7,6},{8,9},{9,8},{10,11... | collective-permute-start | bytes 1572872 | tf_op jit(solution)/shard_map/ppermute | solution.py:157
  61.0 7.6 %collective-permute-done.3.refs_2_ = f32[8,128,128]{2,1,0:T(8,128)} collective-permute-done((f32[8,128,128]{2,1,0:T(8,128)S(1)}, f32[8,128,128]{2,1,0:T(8,128)}, u32[]{:S(2)}, u32[]{:S(2)}) %collective-permute-start.3) | collective-permute-done | bytes 524320 | tf_op jit(solution)/shard_map/ppermute | solution.py:157
  68.6 1.7 %collective-permute-start.4 = (f32[8,128,128]{2,1,0:T(8,128)}, f32[8,128,128]{2,1,0:T(8,128)}, u32[]{:S(2)}, u32[]{:S(2)}) collective-permute-start(f32[8,128,128]{2,1,0:T(8,128)} %collective-permute-done.3.refs_2_), channel_id=1, source_target_pairs={{0,1},{1,0},{2,3},{3,2},{4,5},{5,4},{6,7},{7,6},{8,9},{9,8},{10,11... | collective-permute-start | bytes 1572872 | tf_op jit(solution)/shard_map/ppermute | solution.py:157
  71.7 4.9 %sort.1 = (s32[3,136]{1,0:T(4,128)}, s32[3]{0:T(128)}) custom-call(s32[2,4,3,16]{3,2,1,0:T(4,128)} %bitcast.18, s32[2,4]{1,0:T(2,128)} %bitcast.19), custom_call_target="tpu_custom_call" | custom-call | bytes 4000 | tf_op jit(solution)/shard_map/sort/pallas_call | solution.py:236
  78.7 1.0 %copy-done.6 = f32[8,128,128]{2,1,0:T(8,128)S(1)} copy-done((f32[8,128,128]{2,1,0:T(8,128)S(1)}, f32[8,128,128]{2,1,0:T(8,128)}, u32[]{:S(2)}) %copy-start.6) | copy-done | bytes 524312
  79.8 1.0 %copy-done.8 = f32[8,128,128]{2,1,0:T(8,128)S(1)} copy-done((f32[8,128,128]{2,1,0:T(8,128)S(1)}, f32[8,128,128]{2,1,0:T(8,128)}, u32[]{:S(2)}) %copy-start.8) | copy-done | bytes 524312
  80.8 1.0 %copy-done.10 = f32[8,128,128]{2,1,0:T(8,128)S(1)} copy-done((f32[8,128,128]{2,1,0:T(8,128)S(1)}, f32[8,128,128]{2,1,0:T(8,128)}, u32[]{:S(2)}) %copy-start.10) | copy-done | bytes 524312
  83.2 4.1 %shard_map.46.refs_18_ = f32[32,128,128]{2,1,0:T(8,128)S(1)} custom-call(s32[3]{0:T(128)S(1)} %copy-done.14, s32[3,136]{1,0:T(4,128)S(1)} %copy-done.13, f32[8,128,128]{2,1,0:T(8,128)S(1)} %bitcast.17, f32[8,128,128]{2,1,0:T(8,128)S(1)} %copy-done.6, f32[8,128,128]{2,1,0:T(8,128)S(1)} %copy-done.3, f32[8,128,128]{2,1,0:T(8,128)S(1)} %copy-done.10, ...), custom_call_target="tpu_custom_call" | custom-call | flops 855638016 | bytes 5242880 | tf_op jit(solution)/shard_map/pallas_call | solution.py:128
  87.3 5.3 %shard_map.47.refs_14_ = f32[32,128,128]{2,1,0:T(8,128)S(1)} custom-call(s32[3]{0:T(128)S(1)} %copy-done.14, s32[3,136]{1,0:T(4,128)S(1)} %copy-done.13, f32[8,128,128]{2,1,0:T(8,128)S(1)} %broadcast_select_fusion.refs_2_, f32[8,128,128]{2,1,0:T(8,128)} %collective-permute-done.17.refs_3_, f32[8,128,128]{2,1,0:T(8,128)S(1)} %broadcast_select_fusion.1.refs_4_, ...), custom_call_target="tpu_custom_call" | custom-call | flops 855638016 | bytes 5242880 | tf_op jit(solution)/shard_map/pallas_call | solution.py:128
  92.7 4.3 %shard_map.48 = f32[32,128,128]{2,1,0:T(8,128)} custom-call(s32[3]{0:T(128)S(1)} %copy-done.14, s32[3,136]{1,0:T(4,128)S(1)} %copy-done.13, f32[8,128,128]{2,1,0:T(8,128)} %collective-permute-done.3.refs_2_, f32[8,128,128]{2,1,0:T(8,128)} %collective-permute-done.4.refs_3_, f32[4,128,128]{2,1,0:T(8,128)} %collective-permute-done.6.refs_4_, ...), custom_call_target="tpu_custom_call" | custom-call | flops 855638016 | bytes 5242880 | tf_op jit(solution)/shard_map/pallas_call | solution.py:128
  (63 shorter events, 10.0 us)
Async XLA Ops:
  0.0 14.1 %collective-permute-start = (f32[8,128,128]{2,1,0:T(8,128)}, f32[8,128,128]{2,1,0:T(8,128)S(1)}, u32[]{:S(2)}, u32[]{:S(2)}) collective-permute-start(f32[8,128,128]{2,1,0:T(8,128)} %bitcast.13), channel_id=1, source_target_pairs={{0,4},{4,0},{8,12},{12,8},{1,5},{5,1},{9,13},{13,9},{2,6},{6,2},{1... | collective-permute-start | bytes 1572872 | tf_op jit(solution)/shard_map/ppermute | solution.py:166
  2.1 13.1 %collective-permute-start.15 = (f32[8,128,128]{2,1,0:T(8,128)}, f32[8,128,128]{2,1,0:T(8,128)S(1)}, u32[]{:S(2)}, u32[]{:S(2)}) collective-permute-start(f32[8,128,128]{2,1,0:T(8,128)} %bitcast.14), channel_id=1, source_target_pairs={{0,1},{1,0},{2,3},{3,2},{4,8},{5,9},{6,10},{7,11},{8,4},{9,5},{10,... | collective-permute-start | bytes 1572872 | tf_op jit(solution)/shard_map/ppermute | solution.py:175
  3.1 15.9 %collective-permute-start.5 = (f32[8,128,128]{2,1,0:T(8,128)}, f32[8,128,128]{2,1,0:T(8,128)}, u32[]{:S(2)}, u32[]{:S(2)}) collective-permute-start(f32[8,128,128]{2,1,0:T(8,128)} %bitcast.15), channel_id=1, source_target_pairs={{0,2},{1,3},{2,0},{3,1},{4,6},{5,7},{6,4},{7,5},{8,10},{9,11},{10,... | collective-permute-start | bytes 1572872 | tf_op jit(solution)/shard_map/ppermute | solution.py:157
  14.1 16.9 %copy-start.1 = (f32[8,128,128]{2,1,0:T(8,128)}, f32[8,128,128]{2,1,0:T(8,128)S(1)}, u32[]{:S(2)}) copy-start(f32[8,128,128]{2,1,0:T(8,128)S(1)} %collective-permute-done.refs_4_) | copy-start | bytes 1572868
  14.1 7.5 %collective-permute-start.1 = (f32[8,128,128]{2,1,0:T(8,128)S(1)}, f32[8,128,128]{2,1,0:T(8,128)S(1)}, u32[]{:S(2)}, u32[]{:S(2)}) collective-permute-start(f32[8,128,128]{2,1,0:T(8,128)S(1)} %collective-permute-done.refs_4_), channel_id=1, source_target_pairs={{0,1},{1,0},{2,3},{3,2},{4,8},{5,9},{6,10},{7,11},{8,4},{9,5},{10,... | collective-permute-start | bytes 1572872 | tf_op jit(solution)/shard_map/ppermute | solution.py:175
  15.2 17.4 %collective-permute-start.16 = (f32[8,128,128]{2,1,0:T(8,128)S(1)}, f32[8,128,128]{2,1,0:T(8,128)}, u32[]{:S(2)}, u32[]{:S(2)}) collective-permute-start(f32[8,128,128]{2,1,0:T(8,128)S(1)} %collective-permute-done.15), channel_id=1, source_target_pairs={{0,4},{4,0},{8,12},{12,8},{1,5},{5,1},{9,13},{13,9},{2,6},{6,2},{1... | collective-permute-start | bytes 1572872 | tf_op jit(solution)/shard_map/ppermute | solution.py:166
  16.5 11.9 %collective-permute-start.11 = (f32[4,128,128]{2,1,0:T(8,128)}, f32[4,128,128]{2,1,0:T(8,128)S(1)}, u32[]{:S(2)}, u32[]{:S(2)}) collective-permute-start(f32[4,128,128]{2,1,0:T(8,128)} %bitcast.7), channel_id=1, source_target_pairs={{0,2},{1,3},{2,0},{3,1},{4,6},{5,7},{6,4},{7,5},{8,10},{9,11},{10,... | collective-permute-start | bytes 786440 | tf_op jit(solution)/shard_map/ppermute | solution.py:157
  17.8 13.2 %collective-permute-start.9 = (f32[4,128,128]{2,1,0:T(8,128)}, f32[4,128,128]{2,1,0:T(8,128)S(1)}, u32[]{:S(2)}, u32[]{:S(2)}) collective-permute-start(f32[4,128,128]{2,1,0:T(8,128)} %bitcast.8), channel_id=1, source_target_pairs={{0,16},{16,0},{1,17},{17,1},{2,18},{18,2},{3,19},{19,3},{4,20},{20... | collective-permute-start | bytes 786440 | tf_op jit(solution)/shard_map/ppermute | solution.py:163
  19.0 13.3 %collective-permute-start.8 = (f32[4,128,128]{2,1,0:T(8,128)}, f32[4,128,128]{2,1,0:T(8,128)S(1)}, u32[]{:S(2)}, u32[]{:S(2)}) collective-permute-start(f32[4,128,128]{2,1,0:T(8,128)} %bitcast.9), channel_id=1, source_target_pairs={{0,1},{1,0},{2,3},{3,2},{4,5},{5,4},{6,7},{7,6},{8,9},{9,8},{10,11... | collective-permute-start | bytes 786440 | tf_op jit(solution)/shard_map/ppermute | solution.py:157
  21.5 19.8 %copy-start.15 = (f32[8,128,128]{2,1,0:T(8,128)}, f32[8,128,128]{2,1,0:T(8,128)S(1)}, u32[]{:S(2)}) copy-start(f32[8,128,128]{2,1,0:T(8,128)S(1)} %collective-permute-done.1) | copy-start | bytes 1572868
  21.5 19.8 %collective-permute-start.2 = (f32[8,128,128]{2,1,0:T(8,128)S(1)}, f32[8,128,128]{2,1,0:T(8,128)}, u32[]{:S(2)}, u32[]{:S(2)}) collective-permute-start(f32[8,128,128]{2,1,0:T(8,128)S(1)} %collective-permute-done.1), channel_id=1, source_target_pairs={{0,4},{4,0},{8,12},{12,8},{1,5},{5,1},{9,13},{13,9},{2,6},{6,2},{1... | collective-permute-start | bytes 1572872 | tf_op jit(solution)/shard_map/ppermute | solution.py:166
  27.4 43.7 %copy-start.16 = (s32[1,1,1,2,4,3,16]{6,4,5,3,2,1,0:T(4,128)S(1)}, s32[1,1,1,2,4,3,16]{6,4,5,3,2,1,0:T(4,128)}, u32[]{:S(2)}) copy-start(s32[1,1,1,2,4,3,16]{6,4,5,3,2,1,0:T(4,128)} %param.6) | copy-start | bytes 4612
  27.4 49.2 %copy-start = (f32[4,1,128,128]{3,2,1,0:T(8,128)S(1)}, f32[4,1,128,128]{3,2,1,0:T(8,128)}, u32[]{:S(2)}) copy-start(f32[4,1,128,128]{3,2,1,0:T(8,128)} %param.5) | copy-start | bytes 786436
  28.5 14.3 %collective-permute-start.23 = (f32[8,128,128]{2,1,0:T(8,128)}, f32[8,128,128]{2,1,0:T(8,128)S(1)}, u32[]{:S(2)}, u32[]{:S(2)}) collective-permute-start(f32[8,128,128]{2,1,0:T(8,128)} %bitcast.16), channel_id=1, source_target_pairs={{0,1},{1,0},{2,3},{3,2},{4,5},{5,4},{6,7},{7,6},{8,9},{9,8},{10,11... | collective-permute-start | bytes 1572872 | tf_op jit(solution)/shard_map/ppermute | solution.py:157
  31.0 19.5 %copy-start.2 = (f32[8,128,128]{2,1,0:T(8,128)S(1)}, f32[8,128,128]{2,1,0:T(8,128)}, u32[]{:S(2)}) copy-start(f32[8,128,128]{2,1,0:T(8,128)} %copy-done.1) | copy-start | bytes 1572868
  31.0 8.0 %collective-permute-start.13 = (f32[4,128,128]{2,1,0:T(8,128)S(1)}, f32[4,128,128]{2,1,0:T(8,128)S(1)}, u32[]{:S(2)}, u32[]{:S(2)}) collective-permute-start(f32[4,128,128]{2,1,0:T(8,128)S(1)} %collective-permute-done.11.refs_12_.refs_14_.refs_10_), channel_id=1, source_target_pairs={{0,16},{16,0},{1,17},{17,1},{2,18},{18,2},{3,19},{19,3},{4,20},{20... | collective-permute-start | bytes 786440 | tf_op jit(solution)/shard_map/ppermute | solution.py:163
  32.3 8.0 %collective-permute-start.12 = (f32[4,128,128]{2,1,0:T(8,128)S(1)}, f32[4,128,128]{2,1,0:T(8,128)S(1)}, u32[]{:S(2)}, u32[]{:S(2)}) collective-permute-start(f32[4,128,128]{2,1,0:T(8,128)S(1)} %collective-permute-done.11.refs_12_.refs_14_.refs_10_), channel_id=1, source_target_pairs={{0,1},{1,0},{2,3},{3,2},{4,5},{5,4},{6,7},{7,6},{8,9},{9,8},{10,11... | collective-permute-start | bytes 786440 | tf_op jit(solution)/shard_map/ppermute | solution.py:157
  32.6 8.7 %collective-permute-start.10 = (f32[4,128,128]{2,1,0:T(8,128)S(1)}, f32[4,128,128]{2,1,0:T(8,128)S(1)}, u32[]{:S(2)}, u32[]{:S(2)}) collective-permute-start(f32[4,128,128]{2,1,0:T(8,128)S(1)} %collective-permute-done.9.refs_10_.refs_12_.refs_8_), channel_id=1, source_target_pairs={{0,1},{1,0},{2,3},{3,2},{4,5},{5,4},{6,7},{7,6},{8,9},{9,8},{10,11... | collective-permute-start | bytes 786440 | tf_op jit(solution)/shard_map/ppermute | solution.py:157
  39.0 7.1 %collective-permute-start.19 = (f32[4,128,128]{2,1,0:T(8,128)S(1)}, f32[4,128,128]{2,1,0:T(8,128)S(1)}, u32[]{:S(2)}, u32[]{:S(2)}) collective-permute-start(f32[4,128,128]{2,1,0:T(8,128)S(1)} %slice.9), channel_id=1, source_target_pairs={{0,2},{1,3},{2,0},{3,1},{4,6},{5,7},{6,4},{7,5},{8,10},{9,11},{10,... | collective-permute-start | bytes 786440 | tf_op jit(solution)/shard_map/ppermute | solution.py:157
  40.2 12.1 %collective-permute-start.25 = (f32[8,128,128]{2,1,0:T(8,128)}, f32[8,128,128]{2,1,0:T(8,128)S(1)}, u32[]{:S(2)}, u32[]{:S(2)}) collective-permute-start(f32[8,128,128]{2,1,0:T(8,128)} %collective-permute-done.5.refs_6_), channel_id=1, source_target_pairs={{0,1},{1,0},{2,3},{3,2},{4,5},{5,4},{6,7},{7,6},{8,9},{9,8},{10,11... | collective-permute-start | bytes 1572872 | tf_op jit(solution)/shard_map/ppermute | solution.py:157
  41.3 2.2 %collective-permute-start.14 = (f32[4,128,128]{2,1,0:T(8,128)S(1)}, f32[4,128,128]{2,1,0:T(8,128)S(1)}, u32[]{:S(2)}, u32[]{:S(2)}) collective-permute-start(f32[4,128,128]{2,1,0:T(8,128)S(1)} %collective-permute-done.13.refs_14_.refs_16_.refs_12_), channel_id=1, source_target_pairs={{0,1},{1,0},{2,3},{3,2},{4,5},{5,4},{6,7},{7,6},{8,9},{9,8},{10,11... | collective-permute-start | bytes 786440 | tf_op jit(solution)/shard_map/ppermute | solution.py:157
  41.4 16.0 %collective-permute-start.21 = (f32[8,128,128]{2,1,0:T(8,128)S(1)}, f32[8,128,128]{2,1,0:T(8,128)}, u32[]{:S(2)}, u32[]{:S(2)}) collective-permute-start(f32[8,128,128]{2,1,0:T(8,128)S(1)} %broadcast_select_fusion.refs_2_), channel_id=1, source_target_pairs={{0,2},{1,3},{2,0},{3,1},{4,6},{5,7},{6,4},{7,5},{8,10},{9,11},{10,... | collective-permute-start | bytes 1572872 | tf_op jit(solution)/shard_map/ppermute | solution.py:157
  43.5 7.0 %collective-permute-start.6 = (f32[4,128,128]{2,1,0:T(8,128)S(1)}, f32[4,128,128]{2,1,0:T(8,128)}, u32[]{:S(2)}, u32[]{:S(2)}) collective-permute-start(f32[4,128,128]{2,1,0:T(8,128)S(1)} %slice.8), channel_id=1, source_target_pairs={{0,4},{4,0},{8,12},{12,8},{1,5},{5,1},{9,13},{13,9},{2,6},{6,2},{1... | collective-permute-start | bytes 786440 | tf_op jit(solution)/shard_map/ppermute | solution.py:166
  43.5 25.1 %collective-permute-start.3 = (f32[8,128,128]{2,1,0:T(8,128)S(1)}, f32[8,128,128]{2,1,0:T(8,128)}, u32[]{:S(2)}, u32[]{:S(2)}) collective-permute-start(f32[8,128,128]{2,1,0:T(8,128)S(1)} %broadcast_select_fusion.1.refs_4_), channel_id=1, source_target_pairs={{0,2},{1,3},{2,0},{3,1},{4,6},{5,7},{6,4},{7,5},{8,10},{9,11},{10,... | collective-permute-start | bytes 1572872 | tf_op jit(solution)/shard_map/ppermute | solution.py:157
  46.0 14.2 %collective-permute-start.20 = (f32[4,128,128]{2,1,0:T(8,128)S(1)}, f32[4,128,128]{2,1,0:T(8,128)S(1)}, u32[]{:S(2)}, u32[]{:S(2)}) collective-permute-start(f32[4,128,128]{2,1,0:T(8,128)S(1)} %collective-permute-done.19.refs_6_), channel_id=1, source_target_pairs={{0,1},{1,0},{2,3},{3,2},{4,5},{5,4},{6,7},{7,6},{8,9},{9,8},{10,11... | collective-permute-start | bytes 786440 | tf_op jit(solution)/shard_map/ppermute | solution.py:157
  50.5 19.8 %collective-permute-start.24 = (f32[8,128,128]{2,1,0:T(8,128)S(1)}, f32[8,128,128]{2,1,0:T(8,128)S(1)}, u32[]{:S(2)}, u32[]{:S(2)}) collective-permute-start(f32[8,128,128]{2,1,0:T(8,128)S(1)} %copy-done.2), channel_id=1, source_target_pairs={{0,1},{1,0},{2,3},{3,2},{4,5},{5,4},{6,7},{7,6},{8,9},{9,8},{10,11... | collective-permute-start | bytes 1572872 | tf_op jit(solution)/shard_map/ppermute | solution.py:157
  53.1 34.2 %collective-permute-start.17 = (f32[8,128,128]{2,1,0:T(8,128)S(1)}, f32[8,128,128]{2,1,0:T(8,128)}, u32[]{:S(2)}, u32[]{:S(2)}) collective-permute-start(f32[8,128,128]{2,1,0:T(8,128)S(1)} %broadcast_select_fusion.refs_2_), channel_id=1, source_target_pairs={{0,1},{1,0},{2,3},{3,2},{4,5},{5,4},{6,7},{7,6},{8,9},{9,8},{10,11... | collective-permute-start | bytes 1572872 | tf_op jit(solution)/shard_map/ppermute | solution.py:157
  57.4 29.9 %collective-permute-start.22 = (f32[8,128,128]{2,1,0:T(8,128)}, f32[8,128,128]{2,1,0:T(8,128)}, u32[]{:S(2)}, u32[]{:S(2)}) collective-permute-start(f32[8,128,128]{2,1,0:T(8,128)} %collective-permute-done.21.refs_8_), channel_id=1, source_target_pairs={{0,1},{1,0},{2,3},{3,2},{4,5},{5,4},{6,7},{7,6},{8,9},{9,8},{10,11... | collective-permute-start | bytes 1572872 | tf_op jit(solution)/shard_map/ppermute | solution.py:157
  61.0 26.3 %collective-permute-start.18 = (f32[8,128,128]{2,1,0:T(8,128)S(1)}, f32[8,128,128]{2,1,0:T(8,128)}, u32[]{:S(2)}, u32[]{:S(2)}) collective-permute-start(f32[8,128,128]{2,1,0:T(8,128)S(1)} %broadcast_select_fusion.1.refs_4_), channel_id=1, source_target_pairs={{0,1},{1,0},{2,3},{3,2},{4,5},{5,4},{6,7},{7,6},{8,9},{9,8},{10,11... | collective-permute-start | bytes 1572872 | tf_op jit(solution)/shard_map/ppermute | solution.py:157
  68.6 24.0 %collective-permute-start.4 = (f32[8,128,128]{2,1,0:T(8,128)}, f32[8,128,128]{2,1,0:T(8,128)}, u32[]{:S(2)}, u32[]{:S(2)}) collective-permute-start(f32[8,128,128]{2,1,0:T(8,128)} %collective-permute-done.3.refs_2_), channel_id=1, source_target_pairs={{0,1},{1,0},{2,3},{3,2},{4,5},{5,4},{6,7},{7,6},{8,9},{9,8},{10,11... | collective-permute-start | bytes 1572872 | tf_op jit(solution)/shard_map/ppermute | solution.py:157
  71.1 21.6 %collective-permute-start.7 = (f32[4,128,128]{2,1,0:T(8,128)}, f32[4,128,128]{2,1,0:T(8,128)}, u32[]{:S(2)}, u32[]{:S(2)}) collective-permute-start(f32[4,128,128]{2,1,0:T(8,128)} %collective-permute-done.6.refs_4_), channel_id=1, source_target_pairs={{0,1},{1,0},{2,3},{3,2},{4,5},{5,4},{6,7},{7,6},{8,9},{9,8},{10,11... | collective-permute-start | bytes 786440 | tf_op jit(solution)/shard_map/ppermute | solution.py:157
  83.2 4.2 %copy-start.12 = (f32[4,128,128]{2,1,0:T(8,128)S(1)}, f32[4,128,128]{2,1,0:T(8,128)}, u32[]{:S(2)}) copy-start(f32[4,128,128]{2,1,0:T(8,128)} %copy-done.11) | copy-start | bytes 786436
  (11 other events, 9.6 us)

commit v3 on v2

--- a/solution.py
+++ b/solution.py
@@ -16,7 +16,7 @@
 
 
 def sort_kernel(rel_of, place_of, a_cap, cut, b_of, plan, counts, lists, sizes, stage_tab, base_tab):
-    shards, layers, _, _ = plan.shape
+    shards, _, layers, _ = plan.shape
     n_col = stage_tab.shape[0] // (2 * layers)
     stages = sizes.shape[0]
     z, me = lax.axis_index("col"), lax.axis_index("layer")
@@ -42,13 +42,13 @@
         b_base = b_of(s, row, dm)
 
         def per_pair(p, _):
-            left = plan[s, m, 0, p]
+            left = plan[s, 0, m, p]
             within = left % a_cap
             at = ((left // (layers * a_cap)) * layers + dm) * 2 + jnp.where(within >= cut, 1, 0)
             st = stage_tab[at]
             pos = sizes[st]
             lists[st, pos] = (
-                (base_tab[at] + within) | ((b_base + plan[s, m, 1, p]) << 10) | (plan[s, m, 2, p] << 20)
+                (base_tab[at] + within) | ((b_base + plan[s, 1, m, p]) << 10) | (plan[s, 2, m, p] << 20)
             )
             sizes[st] = pos + 1
             return 0
@@ -175,10 +175,15 @@
         return lax.ppermute(x, ("col", "layer"), moves)
 
     is_end = jnp.logical_or(z == 0, z == n_col - 1)
-    g = a_cap // 2
-    y_own = over_layer(own)
-    p_a = pairs_end(own)
-    p_b = pairs_mid(own)
+    h = a_cap // 2
+    g = a_cap * 3 // 4
+    got = dict(own=own)
+
+    def keep(name, x):
+        got[name] = x
+        return x
+
+    y_own = keep("yown", over_layer(own))
     swapped = n_row == 2
     b_here = b_own if swapped else lax.all_gather(b_own, "row", axis=0, tiled=True)
     y_b = over_layer(b_here)
@@ -187,34 +192,41 @@
         b_rows = dict(b=b_own, xb=x_b, yb=y_b, xyb=over_row(y_b))
     else:
         b_rows = dict(b=b_here, yb=y_b)
-    q = pairs_mid(p_a)
-    r = pairs_end(p_b)
-    y_a = over_layer(p_a[g:])
-    x2 = jnp.where(is_end, r, p_b)
-    y_2 = over_layer(x2)
-    t = pairs_end(q)
-    x3 = jnp.where(is_end, t, q)
-    y_3 = over_layer(x3)
-    p_y = pairs_end(y_own[:g])
-    c_of = {}
-    for name, x in dict(own=own, pa=p_a, yown=y_own, x2=x2, x3=x3, ya=y_a, y2=y_2, py=p_y, y3=y_3).items():
-        c_of[name] = (x, core(x))
+    for i, piece in (("1", own[:h]), ("2", own[h:])):
+        p_a = keep("pa" + i, pairs_end(piece))
+        p_b = pairs_mid(piece)
+        q = pairs_mid(p_a)
+        r = pairs_end(p_b)
+        t = pairs_end(q)
+        x2 = keep("x2" + i, jnp.where(is_end, r, p_b))
+        x3 = keep("x3" + i, jnp.where(is_end, t, q))
+        keep("y2" + i, over_layer(x2))
+        keep("y3" + i, over_layer(x3))
+    keep("ya", over_layer(got["pa2"][g - h :]))
+    keep("py", pairs_end(y_own[:g]))
+    c_of = {name: (x, core(x)) for name, x in got.items()}
 
     stages = [
-        [(0, 0, (0, 1), "own"), (1, 0, (0, 1), "pa"), (0, half, (0, 1), "yown")],
-        [(2, 0, (0, 1), "x2"), (3, 0, (0, 1), "x3"), (1, half, (1,), "ya"), (2, half, (0, 1), "y2")],
-        [(3, half, (0, 1), "y3"), (1, half, (0,), "py")],
+        [(0, 0, (0, 1), ("own",)), (1, 0, (0, 1), ("pa1", "pa2")), (0, half, (0, 1), ("yown",))],
+        [
+            (2, 0, (0, 1), ("x21", "x22")),
+            (3, 0, (0, 1), ("x31", "x32")),
+            (1, half, (1,), ("ya",)),
+            (2, half, (0, 1), ("y21", "y22")),
+        ],
+        [(3, half, (0, 1), ("y31", "y32")), (1, half, (0,), ("py",))],
     ]
     place_of, a_parts = {}, []
     for st, groups in enumerate(stages):
         at, parts = 0, []
-        for rel, dm, halves_here, name in groups:
+        for rel, dm, which, names in groups:
             for other in (0, 1):
-                x = c_of[name][other]
-                for part in halves_here:
-                    place_of[rel, dm ^ other, part] = (st, at - (g if halves_here == (1,) else 0))
-                parts.append((x, at, x.shape[0]))
-                at += x.shape[0]
+                for part in which:
+                    place_of[rel, dm ^ other, part] = (st, at - (g if which == (1,) else 0))
+                for name in names:
+                    x = c_of[name][other]
+                    parts.append((x, at, x.shape[0]))
+                    at += x.shape[0]
         a_parts.append(parts)
 
     b_parts = []
@@ -244,7 +256,7 @@
         scratch_shapes=[pltpu.SMEM((n_col * layers * 2,), jnp.int32)] * 2,
         cost_estimate=pl.CostEstimate(flops=0, bytes_accessed=4000, transcendentals=0),
         name="sort",
-    )(plan, counts)
+    )(plan.transpose(0, 2, 1, 3), counts)
     acc = None
     for st, parts in enumerate(a_parts):
         acc = run_stage(st, sizes, lists, parts, b_parts, acc)

time: 97.6 us -> 97.3 us (level)
  waiting for transfers between devices: 29.6 us -> 19.6 us
  starting transfers between devices: 35.1 us -> 41.3 us
  local copies, waits for them, and re-layouts: 11.3 us -> 14.3 us
    ppermute x2, waiting for transfers between devices: 5.1 us -> 0.01 us  [over_row(): return lax.ppermute(x, 'row', [(i, i ^ 1) for i in range(n_row)])]
    ppermute x18 -> x25, waiting for transfers between devices: 13.2 us -> 8.34 us  [over_layer(): return lax.ppermute(x, 'layer', [(i, i ^ d) for i in range(n_layer)])]
    ppermute x4 -> x7, starting transfers between devices: 9.31 us -> 12.4 us  [pairs_end(): return lax.ppermute(x, 'col', [(i, i ^ 1) for i in range(n_col)])]
    unnamed x35 -> x60, local copies, waits for them, and re-layouts: 10.2 us -> 13.2 us
    ppermute x18 -> x25, starting transfers between devices: 21.2 us -> 23.1 us  [over_layer(): return lax.ppermute(x, 'layer', [(i, i ^ d) for i in range(n_layer)])]
    ppermute x2 -> x4, starting transfers between devices: 2.1 us -> 3.45 us  [pairs_mid(): return lax.ppermute(x, ('col', 'layer'), moves)]
    select_n x2 -> x4, other arithmetic: 2.2 us -> 2.05 us  [the longest x2 1.96 us: multiply(): x2 = keep('x2' + i, jnp.where(is_end, r, p_b))]
    ppermute x4 -> x7, waiting for transfers between devices: 11.3 us -> 11.2 us  [pairs_end(): return lax.ppermute(x, 'col', [(i, i ^ 1) for i in range(n_col)])]
  transfers between devices with their start and end apart: 26 -> 38, of which waited for: 6 -> 8; matrix products, arithmetic and copies ran while one was open for 4% -> 3% of each run, Pallas kernels for 15% -> 15%
where the time goes in v3:
time: 97.3 us; the launch traced here: 96.8 us
  starting transfers between devices  41.3 us (42%)
  waiting for transfers between devices  19.6 us (20%)
  Pallas kernels  19.2 us (20%)
  local copies, waits for them, and re-layouts  14.3 us (15%)
  other arithmetic  2.05 us (2%)
    ppermute x25, starting transfers between devices, over_layer(): return lax.ppermute(x, 'layer', [(i, i ^ d) for i in range(n_layer)])  23.1 us
    pallas_call x3, Pallas kernels, run_stage(): pl.pallas_call(functools.partial(stage_kernel, stage, [(at, n) for _, at,...  14.3 us
    unnamed x60, local copies, waits for them, and re-layouts  13.2 us
    ppermute x7, starting transfers between devices, pairs_end(): return lax.ppermute(x, 'col', [(i, i ^ 1) for i in range(n_col)])  12.4 us
    ppermute x7, waiting for transfers between devices, pairs_end(): return lax.ppermute(x, 'col', [(i, i ^ 1) for i in range(n_col)])  11.2 us
    ppermute x25, waiting for transfers between devices, over_layer(): return lax.ppermute(x, 'layer', [(i, i ^ d) for i in range(n_layer)])  8.34 us
    pallas_call x1, Pallas kernels, multiply(): pl.pallas_call(functools.partial(sort_kernel, rel_of, place_of, a_cap, g,...  4.84 us
    ppermute x4, starting transfers between devices, pairs_mid(): return lax.ppermute(x, ('col', 'layer'), moves)  3.45 us
  transfers between devices with their start and end apart: 38, of which 8 were waited for; matrix products, arithmetic and copies ran while one was open for 3% of the time, Pallas kernels for 15%

profile of v3, /device:TPU:1, one launch (start us, length us, event | category | flops | bytes accessed | tf_op | source)
XLA Modules:
  0.0 96.8 jit_solution(12653411965875894857)
XLA Ops:
  0.0 2.1 %collective-permute-start.16 = (f32[4,128,128]{2,1,0:T(8,128)}, f32[4,128,128]{2,1,0:T(8,128)S(1)}, u32[]{:S(2)}, u32[]{:S(2)}) collective-permute-start(f32[4,128,128]{2,1,0:T(8,128)} %bitcast.11), channel_id=1, source_target_pairs={{0,2},{1,3},{2,0},{3,1},{4,6},{5,7},{6,4},{7,5},{8,10},{9,11},{10,... | collective-permute-start | bytes 786440 | tf_op jit(solution)/shard_map/ppermute | solution.py:157
  2.1 1.2 %collective-permute-start.14 = (f32[4,128,128]{2,1,0:T(8,128)}, f32[4,128,128]{2,1,0:T(8,128)S(1)}, u32[]{:S(2)}, u32[]{:S(2)}) collective-permute-start(f32[4,128,128]{2,1,0:T(8,128)} %bitcast.12), channel_id=1, source_target_pairs={{0,16},{16,0},{1,17},{17,1},{2,18},{18,2},{3,19},{19,3},{4,20},{20... | collective-permute-start | bytes 786440 | tf_op jit(solution)/shard_map/ppermute | solution.py:163
  3.3 1.1 %slice_bitcast_fusion = (f32[4,128,128]{2,1,0:T(8,128)S(1)}, f32[4,128,128]{2,1,0:T(8,128)S(1)}) fusion(f32[1,8,128,128]{3,2,1,0:T(8,128)} %param.4), kind=kLoop, calls=%fused_computation | loop fusion | bytes 1048576 | tf_op jit(solution)/shard_map/slice | solution.py:195
  4.3 1.4 %collective-permute-start.4 = (f32[4,128,128]{2,1,0:T(8,128)S(1)}, f32[4,128,128]{2,1,0:T(8,128)S(1)}, u32[]{:S(2)}, u32[]{:S(2)}) collective-permute-start(f32[4,128,128]{2,1,0:T(8,128)S(1)} %get-tuple-element.9), channel_id=1, source_target_pairs={{0,4},{4,0},{8,12},{12,8},{1,5},{5,1},{9,13},{13,9},{2,6},{6,2},{1... | collective-permute-start | bytes 786440 | tf_op jit(solution)/shard_map/ppermute | solution.py:166
  5.7 1.5 %collective-permute-start.13 = (f32[4,128,128]{2,1,0:T(8,128)}, f32[4,128,128]{2,1,0:T(8,128)S(1)}, u32[]{:S(2)}, u32[]{:S(2)}) collective-permute-start(f32[4,128,128]{2,1,0:T(8,128)} %bitcast.13), channel_id=1, source_target_pairs={{0,1},{1,0},{2,3},{3,2},{4,5},{5,4},{6,7},{7,6},{8,9},{9,8},{10,11... | collective-permute-start | bytes 786440 | tf_op jit(solution)/shard_map/ppermute | solution.py:157
  8.3 1.3 %collective-permute-start.20 = (f32[4,128,128]{2,1,0:T(8,128)S(1)}, f32[4,128,128]{2,1,0:T(8,128)}, u32[]{:S(2)}, u32[]{:S(2)}) collective-permute-start(f32[4,128,128]{2,1,0:T(8,128)S(1)} %get-tuple-element.10), channel_id=1, source_target_pairs={{0,1},{1,0},{2,3},{3,2},{4,8},{5,9},{6,10},{7,11},{8,4},{9,5},{10,... | collective-permute-start | bytes 786440 | tf_op jit(solution)/shard_map/ppermute | solution.py:175
  9.5 1.5 %collective-permute-start.22 = (f32[4,128,128]{2,1,0:T(8,128)S(1)}, f32[4,128,128]{2,1,0:T(8,128)}, u32[]{:S(2)}, u32[]{:S(2)}) collective-permute-start(f32[4,128,128]{2,1,0:T(8,128)S(1)} %get-tuple-element.9), channel_id=1, source_target_pairs={{0,1},{1,0},{2,3},{3,2},{4,8},{5,9},{6,10},{7,11},{8,4},{9,5},{10,... | collective-permute-start | bytes 786440 | tf_op jit(solution)/shard_map/ppermute | solution.py:175
  11.0 1.2 %collective-permute-start.18 = (f32[4,128,128]{2,1,0:T(8,128)S(1)}, f32[4,128,128]{2,1,0:T(8,128)S(1)}, u32[]{:S(2)}, u32[]{:S(2)}) collective-permute-start(f32[4,128,128]{2,1,0:T(8,128)S(1)} %collective-permute-done.16.refs_14_.refs_20_.refs_12_), channel_id=1, source_target_pairs={{0,16},{16,0},{1,17},{17,1},{2,18},{18,2},{3,19},{19,3},{4,20},{20... | collective-permute-start | bytes 786440 | tf_op jit(solution)/shard_map/ppermute | solution.py:163
  12.5 4.1 %collective-permute-done.refs_4_ = f32[4,128,128]{2,1,0:T(8,128)S(1)} collective-permute-done((f32[4,128,128]{2,1,0:T(8,128)S(1)}, f32[4,128,128]{2,1,0:T(8,128)S(1)}, u32[]{:S(2)}, u32[]{:S(2)}) %collective-permute-start) | collective-permute-done | bytes 262176 | tf_op jit(solution)/shard_map/ppermute | solution.py:166
  16.6 2.1 %collective-permute-start.17 = (f32[4,128,128]{2,1,0:T(8,128)S(1)}, f32[4,128,128]{2,1,0:T(8,128)S(1)}, u32[]{:S(2)}, u32[]{:S(2)}) collective-permute-start(f32[4,128,128]{2,1,0:T(8,128)S(1)} %collective-permute-done.16.refs_14_.refs_20_.refs_12_), channel_id=1, source_target_pairs={{0,1},{1,0},{2,3},{3,2},{4,5},{5,4},{6,7},{7,6},{8,9},{9,8},{10,11... | collective-permute-start | bytes 786440 | tf_op jit(solution)/shard_map/ppermute | solution.py:157
  19.3 1.1 %collective-permute-start.36 = (f32[4,128,128]{2,1,0:T(8,128)S(1)}, f32[4,128,128]{2,1,0:T(8,128)S(1)}, u32[]{:S(2)}, u32[]{:S(2)}) collective-permute-start(f32[4,128,128]{2,1,0:T(8,128)S(1)} %collective-permute-done.4.refs_5_), channel_id=1, source_target_pairs={{0,1},{1,0},{2,3},{3,2},{4,5},{5,4},{6,7},{7,6},{8,9},{9,8},{10,11... | collective-permute-start | bytes 786440 | tf_op jit(solution)/shard_map/ppermute | solution.py:157
  24.0 4.8 %collective-permute-start.21 = (f32[4,128,128]{2,1,0:T(8,128)}, f32[4,128,128]{2,1,0:T(8,128)}, u32[]{:S(2)}, u32[]{:S(2)}) collective-permute-start(f32[4,128,128]{2,1,0:T(8,128)} %collective-permute-done.20), channel_id=1, source_target_pairs={{0,4},{4,0},{8,12},{12,8},{1,5},{5,1},{9,13},{13,9},{2,6},{6,2},{1... | collective-permute-start | bytes 786440 | tf_op jit(solution)/shard_map/ppermute | solution.py:166
  28.9 3.7 %collective-permute-done.10.refs_8_ = f32[8,128,128]{2,1,0:T(8,128)S(1)} collective-permute-done((f32[8,128,128]{2,1,0:T(8,128)}, f32[8,128,128]{2,1,0:T(8,128)S(1)}, u32[]{:S(2)}, u32[]{:S(2)}) %collective-permute-start.10) | collective-permute-done | bytes 524320 | tf_op jit(solution)/shard_map/ppermute | solution.py:157
  33.6 1.3 %collective-permute-start.19 = (f32[4,128,128]{2,1,0:T(8,128)S(1)}, f32[4,128,128]{2,1,0:T(8,128)S(1)}, u32[]{:S(2)}, u32[]{:S(2)}) collective-permute-start(f32[4,128,128]{2,1,0:T(8,128)S(1)} %collective-permute-done.18.refs_16_.refs_22_.refs_14_), channel_id=1, source_target_pairs={{0,1},{1,0},{2,3},{3,2},{4,5},{5,4},{6,7},{7,6},{8,9},{9,8},{10,11... | collective-permute-start | bytes 786440 | tf_op jit(solution)/shard_map/ppermute | solution.py:157
  34.9 3.5 %collective-permute-start.6 = (f32[4,128,128]{2,1,0:T(8,128)}, f32[4,128,128]{2,1,0:T(8,128)S(1)}, u32[]{:S(2)}, u32[]{:S(2)}) collective-permute-start(f32[4,128,128]{2,1,0:T(8,128)} %collective-permute-done.5), channel_id=1, source_target_pairs={{0,4},{4,0},{8,12},{12,8},{1,5},{5,1},{9,13},{13,9},{2,6},{6,2},{1... | collective-permute-start | bytes 786440 | tf_op jit(solution)/shard_map/ppermute | solution.py:166
  39.4 1.6 %collective-permute-start.29 = (f32[2,128,128]{2,1,0:T(8,128)S(1)}, f32[2,128,128]{2,1,0:T(8,128)S(1)}, u32[]{:S(2)}, u32[]{:S(2)}) collective-permute-start(f32[2,128,128]{2,1,0:T(8,128)S(1)} %collective-permute-done.28.refs_10_), channel_id=1, source_target_pairs={{0,1},{1,0},{2,3},{3,2},{4,5},{5,4},{6,7},{7,6},{8,9},{9,8},{10,11... | collective-permute-start | bytes 393224 | tf_op jit(solution)/shard_map/ppermute | solution.py:157
  41.0 1.2 %collective-permute-start.30 = (f32[4,128,128]{2,1,0:T(8,128)S(1)}, f32[4,128,128]{2,1,0:T(8,128)}, u32[]{:S(2)}, u32[]{:S(2)}) collective-permute-start(f32[4,128,128]{2,1,0:T(8,128)S(1)} %broadcast_select_fusion.1.refs_2_), channel_id=1, source_target_pairs={{0,2},{1,3},{2,0},{3,1},{4,6},{5,7},{6,4},{7,5},{8,10},{9,11},{10,... | collective-permute-start | bytes 786440 | tf_op jit(solution)/shard_map/ppermute | solution.py:157
  43.9 2.3 %collective-permute-start.24 = (f32[4,128,128]{2,1,0:T(8,128)S(1)}, f32[4,128,128]{2,1,0:T(8,128)S(1)}, u32[]{:S(2)}, u32[]{:S(2)}) collective-permute-start(f32[4,128,128]{2,1,0:T(8,128)S(1)} %broadcast_select_fusion.1.refs_2_), channel_id=1, source_target_pairs={{0,1},{1,0},{2,3},{3,2},{4,5},{5,4},{6,7},{7,6},{8,9},{9,8},{10,11... | collective-permute-start | bytes 786440 | tf_op jit(solution)/shard_map/ppermute | solution.py:157
  46.6 1.5 %collective-permute-start.11 = (f32[6,128,128]{2,1,0:T(8,128)S(1)}, f32[6,128,128]{2,1,0:T(8,128)}, u32[]{:S(2)}, u32[]{:S(2)}) collective-permute-start(f32[6,128,128]{2,1,0:T(8,128)S(1)} %slice.24), channel_id=1, source_target_pairs={{0,4},{4,0},{8,12},{12,8},{1,5},{5,1},{9,13},{13,9},{2,6},{6,2},{1... | collective-permute-start | bytes 1179656 | tf_op jit(solution)/shard_map/ppermute | solution.py:166
  48.1 4.1 %collective-permute-done.2 = f32[4,128,128]{2,1,0:T(8,128)S(1)} collective-permute-done((f32[4,128,128]{2,1,0:T(8,128)}, f32[4,128,128]{2,1,0:T(8,128)S(1)}, u32[]{:S(2)}, u32[]{:S(2)}) %collective-permute-start.2) | collective-permute-done | bytes 262176 | tf_op jit(solution)/shard_map/ppermute | solution.py:166
  52.2 1.7 %collective-permute-start.37 = (f32[8,128,128]{2,1,0:T(8,128)S(1)}, f32[8,128,128]{2,1,0:T(8,128)S(1)}, u32[]{:S(2)}, u32[]{:S(2)}) collective-permute-start(f32[8,128,128]{2,1,0:T(8,128)S(1)} %collective-permute-done.10.refs_8_), channel_id=1, source_target_pairs={{0,1},{1,0},{2,3},{3,2},{4,5},{5,4},{6,7},{7,6},{8,9},{9,8},{10,11... | collective-permute-start | bytes 1572872 | tf_op jit(solution)/shard_map/ppermute | solution.py:157
  56.8 1.2 %collective-permute-start.7 = (f32[4,128,128]{2,1,0:T(8,128)S(1)}, f32[4,128,128]{2,1,0:T(8,128)}, u32[]{:S(2)}, u32[]{:S(2)}) collective-permute-start(f32[4,128,128]{2,1,0:T(8,128)S(1)} %broadcast_select_fusion.2.refs_7_), channel_id=1, source_target_pairs={{0,2},{1,3},{2,0},{3,1},{4,6},{5,7},{6,4},{7,5},{8,10},{9,11},{10,... | collective-permute-start | bytes 786440 | tf_op jit(solution)/shard_map/ppermute | solution.py:157
  58.0 2.6 %collective-permute-done.11.refs_6_ = f32[6,128,128]{2,1,0:T(8,128)} collective-permute-done((f32[6,128,128]{2,1,0:T(8,128)S(1)}, f32[6,128,128]{2,1,0:T(8,128)}, u32[]{:S(2)}, u32[]{:S(2)}) %collective-permute-start.11) | collective-permute-done | bytes 393248 | tf_op jit(solution)/shard_map/ppermute | solution.py:166
  60.6 1.0 %collective-permute-start.3 = (f32[4,128,128]{2,1,0:T(8,128)S(1)}, f32[4,128,128]{2,1,0:T(8,128)}, u32[]{:S(2)}, u32[]{:S(2)}) collective-permute-start(f32[4,128,128]{2,1,0:T(8,128)S(1)} %broadcast_select_fusion.3.refs_6_), channel_id=1, source_target_pairs={{0,2},{1,3},{2,0},{3,1},{4,6},{5,7},{6,4},{7,5},{8,10},{9,11},{10,... | collective-permute-start | bytes 786440 | tf_op jit(solution)/shard_map/ppermute | solution.py:157
  63.2 1.6 %collective-permute-start.12 = (f32[6,128,128]{2,1,0:T(8,128)}, f32[6,128,128]{2,1,0:T(8,128)}, u32[]{:S(2)}, u32[]{:S(2)}) collective-permute-start(f32[6,128,128]{2,1,0:T(8,128)} %collective-permute-done.11.refs_6_), channel_id=1, source_target_pairs={{0,1},{1,0},{2,3},{3,2},{4,5},{5,4},{6,7},{7,6},{8,9},{9,8},{10,11... | collective-permute-start | bytes 1179656 | tf_op jit(solution)/shard_map/ppermute | solution.py:157
  66.7 3.2 %collective-permute-done.3.refs_2_ = f32[4,128,128]{2,1,0:T(8,128)} collective-permute-done((f32[4,128,128]{2,1,0:T(8,128)S(1)}, f32[4,128,128]{2,1,0:T(8,128)}, u32[]{:S(2)}, u32[]{:S(2)}) %collective-permute-start.3) | collective-permute-done | bytes 262176 | tf_op jit(solution)/shard_map/ppermute | solution.py:157
  69.9 1.4 %collective-permute-start.8 = (f32[4,128,128]{2,1,0:T(8,128)}, f32[4,128,128]{2,1,0:T(8,128)}, u32[]{:S(2)}, u32[]{:S(2)}) collective-permute-start(f32[4,128,128]{2,1,0:T(8,128)} %collective-permute-done.3.refs_2_), channel_id=1, source_target_pairs={{0,1},{1,0},{2,3},{3,2},{4,5},{5,4},{6,7},{7,6},{8,9},{9,8},{10,11... | collective-permute-start | bytes 786440 | tf_op jit(solution)/shard_map/ppermute | solution.py:157
  71.3 4.8 %sort.1 = (s32[3,136]{1,0:T(4,128)}, s32[3]{0:T(128)}) custom-call(s32[2,3,4,16]{3,2,1,0:T(4,128)} %bitcast.20, s32[2,4]{1,0:T(2,128)} %bitcast.21), custom_call_target="tpu_custom_call" | custom-call | bytes 4000 | tf_op jit(solution)/shard_map/sort/pallas_call | solution.py:248
  77.1 1.0 %copy-done.11 = f32[8,128,128]{2,1,0:T(8,128)S(1)} copy-done((f32[8,128,128]{2,1,0:T(8,128)S(1)}, f32[8,128,128]{2,1,0:T(8,128)}, u32[]{:S(2)}) %copy-start.11) | copy-done | bytes 524312
  82.3 4.1 %shard_map.46.refs_24_ = f32[32,128,128]{2,1,0:T(8,128)S(1)} custom-call(s32[3]{0:T(128)S(1)} %copy-done.29, s32[3,136]{1,0:T(4,128)S(1)} %copy-done.28, f32[8,128,128]{2,1,0:T(8,128)S(1)} %bitcast.19, f32[8,128,128]{2,1,0:T(8,128)} %collective-permute-done.34.refs_3_, f32[4,128,128]{2,1,0:T(8,128)S(1)} %copy-done.13, f32[4,128,128]{2,1,0:T(8,128)S(1)} %copy-done.9, ...), custom_call_target="tpu_custom_call" | custom-call | flops 855638016 | bytes 5242880 | tf_op jit(solution)/shard_map/pallas_call | solution.py:128
  86.5 5.5 %shard_map.47.refs_16_ = f32[32,128,128]{2,1,0:T(8,128)S(1)} custom-call(s32[3]{0:T(128)S(1)} %copy-done.29, s32[3,136]{1,0:T(4,128)S(1)} %copy-done.28, f32[4,128,128]{2,1,0:T(8,128)S(1)} %broadcast_select_fusion.1.refs_2_, f32[4,128,128]{2,1,0:T(8,128)S(1)} %copy-done.3, f32[4,128,128]{2,1,0:T(8,128)S(1)} %copy-done.19, f32[4,128,128]{2,1,0:T(8,128)S(1)} %copy-done.21, ...), custom_call_target="tpu_custom_call" | custom-call | flops 855638016 | bytes 5242880 | tf_op jit(solution)/shard_map/pallas_call | solution.py:128
  92.0 4.8 %shard_map.48 = f32[32,128,128]{2,1,0:T(8,128)} custom-call(s32[3]{0:T(128)S(1)} %copy-done.29, s32[3,136]{1,0:T(4,128)S(1)} %copy-done.28, f32[4,128,128]{2,1,0:T(8,128)} %collective-permute-done.3.refs_2_, f32[4,128,128]{2,1,0:T(8,128)} %collective-permute-done.7.refs_3_, f32[4,128,128]{2,1,0:T(8,128)} %collective-permute-done.8.refs_4_, ...), custom_call_target="tpu_custom_call" | custom-call | flops 855638016 | bytes 5242880 | tf_op jit(solution)/shard_map/pallas_call | solution.py:128
  (115 shorter events, 21.0 us)
Async XLA Ops:
  0.0 8.3 %collective-permute-start.16 = (f32[4,128,128]{2,1,0:T(8,128)}, f32[4,128,128]{2,1,0:T(8,128)S(1)}, u32[]{:S(2)}, u32[]{:S(2)}) collective-permute-start(f32[4,128,128]{2,1,0:T(8,128)} %bitcast.11), channel_id=1, source_target_pairs={{0,2},{1,3},{2,0},{3,1},{4,6},{5,7},{6,4},{7,5},{8,10},{9,11},{10,... | collective-permute-start | bytes 786440 | tf_op jit(solution)/shard_map/ppermute | solution.py:157
  2.1 7.5 %collective-permute-start.14 = (f32[4,128,128]{2,1,0:T(8,128)}, f32[4,128,128]{2,1,0:T(8,128)S(1)}, u32[]{:S(2)}, u32[]{:S(2)}) collective-permute-start(f32[4,128,128]{2,1,0:T(8,128)} %bitcast.12), channel_id=1, source_target_pairs={{0,16},{16,0},{1,17},{17,1},{2,18},{18,2},{3,19},{19,3},{4,20},{20... | collective-permute-start | bytes 786440 | tf_op jit(solution)/shard_map/ppermute | solution.py:163
  4.3 6.7 %collective-permute-start.4 = (f32[4,128,128]{2,1,0:T(8,128)S(1)}, f32[4,128,128]{2,1,0:T(8,128)S(1)}, u32[]{:S(2)}, u32[]{:S(2)}) collective-permute-start(f32[4,128,128]{2,1,0:T(8,128)S(1)} %get-tuple-element.9), channel_id=1, source_target_pairs={{0,4},{4,0},{8,12},{12,8},{1,5},{5,1},{9,13},{13,9},{2,6},{6,2},{1... | collective-permute-start | bytes 786440 | tf_op jit(solution)/shard_map/ppermute | solution.py:166
  5.7 6.5 %collective-permute-start.13 = (f32[4,128,128]{2,1,0:T(8,128)}, f32[4,128,128]{2,1,0:T(8,128)S(1)}, u32[]{:S(2)}, u32[]{:S(2)}) collective-permute-start(f32[4,128,128]{2,1,0:T(8,128)} %bitcast.13), channel_id=1, source_target_pairs={{0,1},{1,0},{2,3},{3,2},{4,5},{5,4},{6,7},{7,6},{8,9},{9,8},{10,11... | collective-permute-start | bytes 786440 | tf_op jit(solution)/shard_map/ppermute | solution.py:157
  7.2 9.4 %collective-permute-start = (f32[4,128,128]{2,1,0:T(8,128)S(1)}, f32[4,128,128]{2,1,0:T(8,128)S(1)}, u32[]{:S(2)}, u32[]{:S(2)}) collective-permute-start(f32[4,128,128]{2,1,0:T(8,128)S(1)} %get-tuple-element.10), channel_id=1, source_target_pairs={{0,4},{4,0},{8,12},{12,8},{1,5},{5,1},{9,13},{13,9},{2,6},{6,2},{1... | collective-permute-start | bytes 786440 | tf_op jit(solution)/shard_map/ppermute | solution.py:166
  8.3 10.5 %collective-permute-start.20 = (f32[4,128,128]{2,1,0:T(8,128)S(1)}, f32[4,128,128]{2,1,0:T(8,128)}, u32[]{:S(2)}, u32[]{:S(2)}) collective-permute-start(f32[4,128,128]{2,1,0:T(8,128)S(1)} %get-tuple-element.10), channel_id=1, source_target_pairs={{0,1},{1,0},{2,3},{3,2},{4,8},{5,9},{6,10},{7,11},{8,4},{9,5},{10,... | collective-permute-start | bytes 786440 | tf_op jit(solution)/shard_map/ppermute | solution.py:175
  9.5 9.4 %collective-permute-start.22 = (f32[4,128,128]{2,1,0:T(8,128)S(1)}, f32[4,128,128]{2,1,0:T(8,128)}, u32[]{:S(2)}, u32[]{:S(2)}) collective-permute-start(f32[4,128,128]{2,1,0:T(8,128)S(1)} %get-tuple-element.9), channel_id=1, source_target_pairs={{0,1},{1,0},{2,3},{3,2},{4,8},{5,9},{6,10},{7,11},{8,4},{9,5},{10,... | collective-permute-start | bytes 786440 | tf_op jit(solution)/shard_map/ppermute | solution.py:175
  11.0 9.4 %collective-permute-start.18 = (f32[4,128,128]{2,1,0:T(8,128)S(1)}, f32[4,128,128]{2,1,0:T(8,128)S(1)}, u32[]{:S(2)}, u32[]{:S(2)}) collective-permute-start(f32[4,128,128]{2,1,0:T(8,128)S(1)} %collective-permute-done.16.refs_14_.refs_20_.refs_12_), channel_id=1, source_target_pairs={{0,16},{16,0},{1,17},{17,1},{2,18},{18,2},{3,19},{19,3},{4,20},{20... | collective-permute-start | bytes 786440 | tf_op jit(solution)/shard_map/ppermute | solution.py:163
  12.2 7.0 %collective-permute-start.28 = (f32[2,128,128]{2,1,0:T(8,128)S(1)}, f32[2,128,128]{2,1,0:T(8,128)S(1)}, u32[]{:S(2)}, u32[]{:S(2)}) collective-permute-start(f32[2,128,128]{2,1,0:T(8,128)S(1)} %slice.25), channel_id=1, source_target_pairs={{0,2},{1,3},{2,0},{3,1},{4,6},{5,7},{6,4},{7,5},{8,10},{9,11},{10,... | collective-permute-start | bytes 393224 | tf_op jit(solution)/shard_map/ppermute | solution.py:157
  18.7 13.8 %collective-permute-start.10 = (f32[8,128,128]{2,1,0:T(8,128)}, f32[8,128,128]{2,1,0:T(8,128)S(1)}, u32[]{:S(2)}, u32[]{:S(2)}) collective-permute-start(f32[8,128,128]{2,1,0:T(8,128)} %bitcast.17), channel_id=1, source_target_pairs={{0,2},{1,3},{2,0},{3,1},{4,6},{5,7},{6,4},{7,5},{8,10},{9,11},{10,... | collective-permute-start | bytes 1572872 | tf_op jit(solution)/shard_map/ppermute | solution.py:157
  21.2 18.1 %collective-permute-start.34 = (f32[8,128,128]{2,1,0:T(8,128)}, f32[8,128,128]{2,1,0:T(8,128)}, u32[]{:S(2)}, u32[]{:S(2)}) collective-permute-start(f32[8,128,128]{2,1,0:T(8,128)} %bitcast.18), channel_id=1, source_target_pairs={{0,1},{1,0},{2,3},{3,2},{4,5},{5,4},{6,7},{7,6},{8,9},{9,8},{10,11... | collective-permute-start | bytes 1572872 | tf_op jit(solution)/shard_map/ppermute | solution.py:157
  21.2 12.4 %collective-permute-start.5 = (f32[4,128,128]{2,1,0:T(8,128)S(1)}, f32[4,128,128]{2,1,0:T(8,128)}, u32[]{:S(2)}, u32[]{:S(2)}) collective-permute-start(f32[4,128,128]{2,1,0:T(8,128)S(1)} %collective-permute-done.4.refs_5_), channel_id=1, source_target_pairs={{0,1},{1,0},{2,3},{3,2},{4,8},{5,9},{6,10},{7,11},{8,4},{9,5},{10,... | collective-permute-start | bytes 786440 | tf_op jit(solution)/shard_map/ppermute | solution.py:175
  22.4 12.5 %collective-permute-start.1 = (f32[4,128,128]{2,1,0:T(8,128)S(1)}, f32[4,128,128]{2,1,0:T(8,128)}, u32[]{:S(2)}, u32[]{:S(2)}) collective-permute-start(f32[4,128,128]{2,1,0:T(8,128)S(1)} %collective-permute-done.refs_4_), channel_id=1, source_target_pairs={{0,1},{1,0},{2,3},{3,2},{4,8},{5,9},{6,10},{7,11},{8,4},{9,5},{10,... | collective-permute-start | bytes 786440 | tf_op jit(solution)/shard_map/ppermute | solution.py:175
  24.0 14.3 %collective-permute-start.21 = (f32[4,128,128]{2,1,0:T(8,128)}, f32[4,128,128]{2,1,0:T(8,128)}, u32[]{:S(2)}, u32[]{:S(2)}) collective-permute-start(f32[4,128,128]{2,1,0:T(8,128)} %collective-permute-done.20), channel_id=1, source_target_pairs={{0,4},{4,0},{8,12},{12,8},{1,5},{5,1},{9,13},{13,9},{2,6},{6,2},{1... | collective-permute-start | bytes 786440 | tf_op jit(solution)/shard_map/ppermute | solution.py:166
  32.5 8.4 %collective-permute-start.23 = (f32[4,128,128]{2,1,0:T(8,128)}, f32[4,128,128]{2,1,0:T(8,128)}, u32[]{:S(2)}, u32[]{:S(2)}) collective-permute-start(f32[4,128,128]{2,1,0:T(8,128)} %collective-permute-done.22), channel_id=1, source_target_pairs={{0,4},{4,0},{8,12},{12,8},{1,5},{5,1},{9,13},{13,9},{2,6},{6,2},{1... | collective-permute-start | bytes 786440 | tf_op jit(solution)/shard_map/ppermute | solution.py:166
  33.6 12.7 %collective-permute-start.19 = (f32[4,128,128]{2,1,0:T(8,128)S(1)}, f32[4,128,128]{2,1,0:T(8,128)S(1)}, u32[]{:S(2)}, u32[]{:S(2)}) collective-permute-start(f32[4,128,128]{2,1,0:T(8,128)S(1)} %collective-permute-done.18.refs_16_.refs_22_.refs_14_), channel_id=1, source_target_pairs={{0,1},{1,0},{2,3},{3,2},{4,5},{5,4},{6,7},{7,6},{8,9},{9,8},{10,11... | collective-permute-start | bytes 786440 | tf_op jit(solution)/shard_map/ppermute | solution.py:157
  34.9 11.7 %collective-permute-start.6 = (f32[4,128,128]{2,1,0:T(8,128)}, f32[4,128,128]{2,1,0:T(8,128)S(1)}, u32[]{:S(2)}, u32[]{:S(2)}) collective-permute-start(f32[4,128,128]{2,1,0:T(8,128)} %collective-permute-done.5), channel_id=1, source_target_pairs={{0,4},{4,0},{8,12},{12,8},{1,5},{5,1},{9,13},{13,9},{2,6},{6,2},{1... | collective-permute-start | bytes 786440 | tf_op jit(solution)/shard_map/ppermute | solution.py:166
  38.3 13.9 %collective-permute-start.2 = (f32[4,128,128]{2,1,0:T(8,128)}, f32[4,128,128]{2,1,0:T(8,128)S(1)}, u32[]{:S(2)}, u32[]{:S(2)}) collective-permute-start(f32[4,128,128]{2,1,0:T(8,128)} %collective-permute-done.1), channel_id=1, source_target_pairs={{0,4},{4,0},{8,12},{12,8},{1,5},{5,1},{9,13},{13,9},{2,6},{6,2},{1... | collective-permute-start | bytes 786440 | tf_op jit(solution)/shard_map/ppermute | solution.py:166
  41.0 13.0 %collective-permute-start.30 = (f32[4,128,128]{2,1,0:T(8,128)S(1)}, f32[4,128,128]{2,1,0:T(8,128)}, u32[]{:S(2)}, u32[]{:S(2)}) collective-permute-start(f32[4,128,128]{2,1,0:T(8,128)S(1)} %broadcast_select_fusion.1.refs_2_), channel_id=1, source_target_pairs={{0,2},{1,3},{2,0},{3,1},{4,6},{5,7},{6,4},{7,5},{8,10},{9,11},{10,... | collective-permute-start | bytes 786440 | tf_op jit(solution)/shard_map/ppermute | solution.py:157
  43.9 11.5 %collective-permute-start.24 = (f32[4,128,128]{2,1,0:T(8,128)S(1)}, f32[4,128,128]{2,1,0:T(8,128)S(1)}, u32[]{:S(2)}, u32[]{:S(2)}) collective-permute-start(f32[4,128,128]{2,1,0:T(8,128)S(1)} %broadcast_select_fusion.1.refs_2_), channel_id=1, source_target_pairs={{0,1},{1,0},{2,3},{3,2},{4,5},{5,4},{6,7},{7,6},{8,9},{9,8},{10,11... | collective-permute-start | bytes 786440 | tf_op jit(solution)/shard_map/ppermute | solution.py:157
  46.3 8.4 %collective-permute-start.31 = (f32[4,128,128]{2,1,0:T(8,128)S(1)}, f32[4,128,128]{2,1,0:T(8,128)}, u32[]{:S(2)}, u32[]{:S(2)}) collective-permute-start(f32[4,128,128]{2,1,0:T(8,128)S(1)} %broadcast_select_fusion.refs_3_), channel_id=1, source_target_pairs={{0,2},{1,3},{2,0},{3,1},{4,6},{5,7},{6,4},{7,5},{8,10},{9,11},{10,... | collective-permute-start | bytes 786440 | tf_op jit(solution)/shard_map/ppermute | solution.py:157
  46.6 14.0 %collective-permute-start.11 = (f32[6,128,128]{2,1,0:T(8,128)S(1)}, f32[6,128,128]{2,1,0:T(8,128)}, u32[]{:S(2)}, u32[]{:S(2)}) collective-permute-start(f32[6,128,128]{2,1,0:T(8,128)S(1)} %slice.24), channel_id=1, source_target_pairs={{0,4},{4,0},{8,12},{12,8},{1,5},{5,1},{9,13},{13,9},{2,6},{6,2},{1... | collective-permute-start | bytes 1179656 | tf_op jit(solution)/shard_map/ppermute | solution.py:166
  52.2 10.2 %collective-permute-start.37 = (f32[8,128,128]{2,1,0:T(8,128)S(1)}, f32[8,128,128]{2,1,0:T(8,128)S(1)}, u32[]{:S(2)}, u32[]{:S(2)}) collective-permute-start(f32[8,128,128]{2,1,0:T(8,128)S(1)} %collective-permute-done.10.refs_8_), channel_id=1, source_target_pairs={{0,1},{1,0},{2,3},{3,2},{4,5},{5,4},{6,7},{7,6},{8,9},{9,8},{10,11... | collective-permute-start | bytes 1572872 | tf_op jit(solution)/shard_map/ppermute | solution.py:157
  54.7 10.1 %collective-permute-start.27 = (f32[4,128,128]{2,1,0:T(8,128)S(1)}, f32[4,128,128]{2,1,0:T(8,128)S(1)}, u32[]{:S(2)}, u32[]{:S(2)}) collective-permute-start(f32[4,128,128]{2,1,0:T(8,128)S(1)} %broadcast_select_fusion.2.refs_7_), channel_id=1, source_target_pairs={{0,1},{1,0},{2,3},{3,2},{4,5},{5,4},{6,7},{7,6},{8,9},{9,8},{10,11... | collective-permute-start | bytes 786440 | tf_op jit(solution)/shard_map/ppermute | solution.py:157
  56.1 9.4 %collective-permute-start.26 = (f32[4,128,128]{2,1,0:T(8,128)S(1)}, f32[4,128,128]{2,1,0:T(8,128)S(1)}, u32[]{:S(2)}, u32[]{:S(2)}) collective-permute-start(f32[4,128,128]{2,1,0:T(8,128)S(1)} %broadcast_select_fusion.3.refs_6_), channel_id=1, source_target_pairs={{0,1},{1,0},{2,3},{3,2},{4,5},{5,4},{6,7},{7,6},{8,9},{9,8},{10,11... | collective-permute-start | bytes 786440 | tf_op jit(solution)/shard_map/ppermute | solution.py:157
  56.8 9.9 %collective-permute-start.7 = (f32[4,128,128]{2,1,0:T(8,128)S(1)}, f32[4,128,128]{2,1,0:T(8,128)}, u32[]{:S(2)}, u32[]{:S(2)}) collective-permute-start(f32[4,128,128]{2,1,0:T(8,128)S(1)} %broadcast_select_fusion.2.refs_7_), channel_id=1, source_target_pairs={{0,2},{1,3},{2,0},{3,1},{4,6},{5,7},{6,4},{7,5},{8,10},{9,11},{10,... | collective-permute-start | bytes 786440 | tf_op jit(solution)/shard_map/ppermute | solution.py:157
  60.6 9.3 %collective-permute-start.3 = (f32[4,128,128]{2,1,0:T(8,128)S(1)}, f32[4,128,128]{2,1,0:T(8,128)}, u32[]{:S(2)}, u32[]{:S(2)}) collective-permute-start(f32[4,128,128]{2,1,0:T(8,128)S(1)} %broadcast_select_fusion.3.refs_6_), channel_id=1, source_target_pairs={{0,2},{1,3},{2,0},{3,1},{4,6},{5,7},{6,4},{7,5},{8,10},{9,11},{10,... | collective-permute-start | bytes 786440 | tf_op jit(solution)/shard_map/ppermute | solution.py:157
  63.2 28.8 %collective-permute-start.12 = (f32[6,128,128]{2,1,0:T(8,128)}, f32[6,128,128]{2,1,0:T(8,128)}, u32[]{:S(2)}, u32[]{:S(2)}) collective-permute-start(f32[6,128,128]{2,1,0:T(8,128)} %collective-permute-done.11.refs_6_), channel_id=1, source_target_pairs={{0,1},{1,0},{2,3},{3,2},{4,5},{5,4},{6,7},{7,6},{8,9},{9,8},{10,11... | collective-permute-start | bytes 1179656 | tf_op jit(solution)/shard_map/ppermute | solution.py:157
  65.5 20.9 %collective-permute-start.32 = (f32[4,128,128]{2,1,0:T(8,128)}, f32[4,128,128]{2,1,0:T(8,128)}, u32[]{:S(2)}, u32[]{:S(2)}) collective-permute-start(f32[4,128,128]{2,1,0:T(8,128)} %collective-permute-done.30.refs_12_), channel_id=1, source_target_pairs={{0,1},{1,0},{2,3},{3,2},{4,5},{5,4},{6,7},{7,6},{8,9},{9,8},{10,11... | collective-permute-start | bytes 786440 | tf_op jit(solution)/shard_map/ppermute | solution.py:157
  66.2 20.2 %collective-permute-start.33 = (f32[4,128,128]{2,1,0:T(8,128)}, f32[4,128,128]{2,1,0:T(8,128)}, u32[]{:S(2)}, u32[]{:S(2)}) collective-permute-start(f32[4,128,128]{2,1,0:T(8,128)} %collective-permute-done.31.refs_13_), channel_id=1, source_target_pairs={{0,1},{1,0},{2,3},{3,2},{4,5},{5,4},{6,7},{7,6},{8,9},{9,8},{10,11... | collective-permute-start | bytes 786440 | tf_op jit(solution)/shard_map/ppermute | solution.py:157
  66.7 25.2 %collective-permute-start.9 = (f32[4,128,128]{2,1,0:T(8,128)}, f32[4,128,128]{2,1,0:T(8,128)}, u32[]{:S(2)}, u32[]{:S(2)}) collective-permute-start(f32[4,128,128]{2,1,0:T(8,128)} %collective-permute-done.7.refs_3_), channel_id=1, source_target_pairs={{0,1},{1,0},{2,3},{3,2},{4,5},{5,4},{6,7},{7,6},{8,9},{9,8},{10,11... | collective-permute-start | bytes 786440 | tf_op jit(solution)/shard_map/ppermute | solution.py:157
  69.9 22.0 %collective-permute-start.8 = (f32[4,128,128]{2,1,0:T(8,128)}, f32[4,128,128]{2,1,0:T(8,128)}, u32[]{:S(2)}, u32[]{:S(2)}) collective-permute-start(f32[4,128,128]{2,1,0:T(8,128)} %collective-permute-done.3.refs_2_), channel_id=1, source_target_pairs={{0,1},{1,0},{2,3},{3,2},{4,5},{5,4},{6,7},{7,6},{8,9},{9,8},{10,11... | collective-permute-start | bytes 786440 | tf_op jit(solution)/shard_map/ppermute | solution.py:157
  (36 other events, 255.0 us)
